TPU v7x, 512 devices: a whole 4x4x16 slice. The times are simulated.
512 devices in a mesh: group: 16 (over x, y), dev: 32 (over z, core).
Axes of the slice: x: 4, y: 4, z: 16, core: 2. Of those that a mesh axis runs over, the one named last changes fastest.
Arguments:
- embeddings: bfloat16 [655360, 768], P(('group', 'dev')), may hold values from -6 to 6
- projection: bfloat16 [256, 768], replicated, may hold values from -0.21875 to 0.21875
- triplets: int32 [3, 1048576], P(None, ('group', 'dev')), may hold values from 0 to 3327, as said below
- cotangent: float32 [1048576], P(('group', 'dev')), may hold values from -24 to 24
- wanted_rows: int32 [8192, 128], P(('group', 'dev')), may hold values from -1 to 1279, as said below
Outputs:
- row_grad: bfloat16 [655360, 768], P(('group', 'dev'))
- weight_grad: float32 [256, 768], replicated
Inputs may be any that keep to these rules, and one draw needn't show every extreme that they name: `wanted_rows`: in each list the live entries come first and are distinct rows of the owning device, the rest are -1; each list holds from 128 // 4 (at least 1) to 128 live entries; all lists of some group of requesters are full, and all lists sent to some group are full. `triplets`: anchors are below 1280; a positive or negative below 1280 is one of the device's own rows, else 1280 + h * 128 + s names a live slot s of the device's list for group h.
All inputs are finite; a program needn't handle non-finite values.
Results may differ from a plain program's by a relative error of at most 0.0058.
Values may be sent and summed in bfloat16 or wider, within the bound.
No kernel may reach another device: no remote copies, remote signals or barrier semaphores. Data moves between devices by JAX's collectives and lax.ppermute only.
A program may use at most 64 MiB of HBM per device.

v0:
```python
import math

import jax
import jax.numpy as jnp
from jax import lax
from jax.sharding import PartitionSpec as P

distance_scale = 0.0625
margin = 1.0
pull_share = 0.5


def triplet_gradients(lookup, triple, cotangent):
    anchor_rows = lookup[triple[0]].astype(jnp.float32)
    positive_rows = lookup[triple[1]].astype(jnp.float32)
    negative_rows = lookup[triple[2]].astype(jnp.float32)
    to_positive = anchor_rows - positive_rows
    to_negative = anchor_rows - negative_rows
    near = distance_scale * jnp.sum(to_positive * to_positive, axis=1)
    far = distance_scale * jnp.sum(to_negative * to_negative, axis=1)
    hinge_gate = jax.nn.sigmoid(margin + near - far)
    pull_factor = 2.0 * distance_scale * cotangent * (1.0 - pull_share + pull_share * hinge_gate)
    push_factor = 2.0 * distance_scale * cotangent * pull_share * hinge_gate
    pull_term = pull_factor[:, None] * to_positive
    push_term = push_factor[:, None] * to_negative
    gradient = jnp.zeros(lookup.shape, jnp.float32)
    gradient = gradient.at[triple[0]].add(pull_term - push_term)
    gradient = gradient.at[triple[1]].add(-pull_term)
    gradient = gradient.at[triple[2]].add(push_term)
    return gradient


def local(embeddings, projection, triplets, cotangent, wanted_rows):
    shard_rows = embeddings.shape[0]
    rank_width = projection.shape[0]
    groups = lax.axis_size("group")
    contract = (((1,), (1,)), ((), ()))
    own_projected = lax.dot_general(
        embeddings, projection, contract, preferred_element_type=jnp.float32
    ).astype(jnp.bfloat16)
    wanted = lax.all_to_all(wanted_rows, "group", split_axis=0, concat_axis=0, tiled=True)
    served_index = jnp.maximum(wanted, 0)
    served = own_projected[served_index]
    fetched = lax.all_to_all(served, "group", split_axis=0, concat_axis=0, tiled=True)
    lookup = jnp.concatenate([own_projected, fetched.reshape(-1, rank_width)], axis=0)
    gradient = triplet_gradients(lookup, triplets, cotangent)
    remote_grad = gradient[shard_rows:].reshape(groups, -1, rank_width).astype(jnp.bfloat16)
    returned = lax.all_to_all(remote_grad, "group", split_axis=0, concat_axis=0, tiled=True)
    row_total = (
        gradient[:shard_rows]
        .at[served_index.reshape(-1)]
        .add(returned.reshape(-1, rank_width).astype(jnp.float32))
    )
    row_rounded = row_total.astype(jnp.bfloat16)
    row_grad = jnp.dot(row_rounded, projection, preferred_element_type=jnp.float32).astype(
        jnp.bfloat16
    )
    partial_value = lax.dot_general(
        row_rounded, embeddings, (((0,), (0,)), ((), ())), preferred_element_type=jnp.float32
    )
    factor = 1.0 / math.sqrt(cotangent.shape[0] * groups * lax.axis_size("dev"))
    weight_total = lax.psum(partial_value, ("group", "dev"))
    return (row_grad, weight_total * factor)


def solution(mesh):
    return jax.shard_map(
        local,
        mesh=mesh,
        in_specs=(
            P(("group", "dev"), None),
            P(),
            P(None, ("group", "dev")),
            P(("group", "dev")),
            P(("group", "dev"), None),
        ),
        out_specs=(P(("group", "dev"), None), P()),
        check_vma=False,
    )
```

profile of v0, /device:TPU:1, one launch (start us, length us, event | category | flops | bytes accessed | tf_op | source)
XLA Modules:
  0.0 647.8 jit_solution(12373123322807966387)
XLA Ops:
  7.2 0.0 copy-start
  7.2 7.7 %all-to-all-start = ((s32[16,1,128]{2,1,0:T(1,128)}), s32[16,1,128]{2,1,0:T(1,128)S(1)}, u32[]{:S(2)}, u32[]{:S(2)}) async-start(s32[16,1,128]{2,1,0:T(1,128)} %bitcast.29), calls=%async_computation | async-start | bytes 16384 | tf_op jit(solution)/shard_map/all_to_all | solution.py:41
  14.9 0.0 copy-done
  14.9 1.7 convolution_convert_fusion.1
  16.6 4.6 all-to-all-done
  21.3 9.1 %gather_fusion = bf16[2048,256]{1,0:T(8,128)(2,1)} fusion(bf16[1280,256]{1,0:T(8,128)(2,1)S(1)} %convolution_convert_fusion.1, s32[2048]{0:T(1024)S(1)} %broadcast_clamp_fusion.3), kind=kCustom, calls=%fused_computation | custom fusion | bytes 2105344 | tf_op jit(solution)/shard_map/gather | solution.py:43
  30.3 0.0 copy-start.1
  30.3 4.5 all-to-all-start.1
  34.8 0.0 copy-done.1
  34.9 12.3 %all-to-all-done.1 = bf16[16,128,256]{2,1,0:T(8,128)(2,1)} async-done(((bf16[16,128,256]{2,1,0:T(8,128)(2,1)}), bf16[16,128,256]{2,1,0:T(8,128)(2,1)}, u32[]{:S(2)}, u32[]{:S(2)}) %all-to-all-start.1) | async-done | bytes 1048608 | tf_op jit(solution)/shard_map/all_to_all | solution.py:44
  47.2 2.5 pad_maximum_fusion
  49.7 8.3 %gather_fusion.1 = bf16[2048,256]{1,0:T(8,128)(2,1)S(1)} fusion(bf16[3328,256]{1,0:T(8,128)(2,1)} %pad_maximum_fusion, s32[2048]{0:T(1024)S(1)} %broadcast_clamp_fusion.2), kind=kCustom, calls=%fused_computation.1 | custom fusion | bytes 2105344 | tf_op jit(solution)/shard_map/gather | solution.py:14
  58.0 10.1 %gather_fusion.3 = bf16[2048,256]{1,0:T(8,128)(2,1)} fusion(bf16[3328,256]{1,0:T(8,128)(2,1)} %pad_maximum_fusion, s32[2048]{0:T(1024)S(1)} %broadcast_clamp_fusion), kind=kCustom, calls=%fused_computation.3 | custom fusion | bytes 2105344 | tf_op jit(solution)/shard_map/gather | solution.py:16
  68.1 10.1 %gather_fusion.2 = bf16[2048,256]{1,0:T(8,128)(2,1)} fusion(bf16[3328,256]{1,0:T(8,128)(2,1)} %pad_maximum_fusion, s32[2048]{0:T(1024)S(1)} %broadcast_clamp_fusion.1), kind=kCustom, calls=%fused_computation.2 | custom fusion | bytes 2105344 | tf_op jit(solution)/shard_map/gather | solution.py:15
  78.2 0.0 copy-start.2
  78.2 2.5 multiply_reduce_fusion.1
  80.7 0.0 copy-done.2
  80.8 15.1 %scatter_custom_fusion = f32[3328,256]{1,0:T(8,128)} fusion(s32[2048]{0:T(1024)S(1)} %bitcast.28, bf16[2048,256]{1,0:T(8,128)(2,1)} %gather_fusion.3, bf16[2048,256]{1,0:T(8,128)(2,1)S(1)} %gather_fusion.1, bf16[2048,256]{1,0:T(8,128)(2,1)} %gather_fusion.2, f32[]{:T(128)} %constant.8.clone.1, f32[2048]{0:T(1024)S(1)} %get-tuple-element.8, ...), kind=kCustom, calls=%fused_computation.17 | custom fusion | flops 4718592 | bytes 6569988 | tf_op jit(solution)/shard_map/scatter-add | solution.py:27
  95.9 16.7 %scatter_custom_fusion.1 = f32[3328,256]{1,0:T(8,128)} fusion(f32[3328,256]{1,0:T(8,128)} %scatter_custom_fusion, s32[2048]{0:T(1024)S(1)} %bitcast.26, bf16[2048,256]{1,0:T(8,128)(2,1)} %gather_fusion.2, bf16[2048,256]{1,0:T(8,128)(2,1)S(1)} %gather_fusion.1, f32[2048]{0:T(1024)S(1)} %get-tuple-element.7), kind=kCustom, calls=%fused_computation.15 | custom fusion | flops 3145728 | bytes 5513216 | tf_op jit(solution)/shard_map/scatter-add | solution.py:28
  112.6 16.6 %scatter_custom_fusion.2 = f32[3328,256]{1,0:T(8,128)} fusion(f32[3328,256]{1,0:T(8,128)} %scatter_custom_fusion.1, s32[2048]{0:T(1024)S(1)} %bitcast.24, bf16[2048,256]{1,0:T(8,128)(2,1)} %gather_fusion.3, bf16[2048,256]{1,0:T(8,128)(2,1)S(1)} %gather_fusion.1, f32[2048]{0:T(1024)S(1)} %get-tuple-element.8), kind=kCustom, calls=%fused_computation.23 | custom fusion | flops 2621440 | bytes 5513216 | tf_op jit(solution)/shard_map/scatter-add | solution.py:29
  129.2 2.7 slice.38
  131.9 4.4 all-to-all-start.2
  136.2 0.0 all-reduce.2.cloned.1.call-start
  136.3 1.4 slice.32
  137.7 10.4 %all-to-all-done.2 = bf16[16,128,256]{2,1,0:T(8,128)(2,1)} async-done(((bf16[16,128,256]{2,1,0:T(8,128)(2,1)}), bf16[16,128,256]{2,1,0:T(8,128)(2,1)}, u32[]{:S(2)}, u32[]{:S(2)}) %all-to-all-start.2) | async-done | bytes 1048608 | tf_op jit(solution)/shard_map/all_to_all | solution.py:48
  148.1 13.4 %scatter_custom_fusion.3 = f32[1280,256]{1,0:T(8,128)S(1)} fusion(f32[1280,256]{1,0:T(8,128)S(1)} %slice.32, s32[2048]{0:T(1024)S(1)} %bitcast.22, bf16[2048,256]{1,0:T(8,128)(2,1)} %bitcast.12), kind=kCustom, calls=%fused_computation.13 | custom fusion | flops 1048576 | bytes 2359296 | tf_op jit(solution)/shard_map/scatter-add | solution.py:52
  161.6 1.6 fusion.18
  163.2 0.0 all-reduce.2.cloned.1.call-update
  163.2 2.9 convolution_convert_fusion
  166.2 472.7 %all-reduce.2.cloned.1.call-done = f32[256,768]{1,0:T(8,128)} async-done(((f32[256,768]{1,0:T(8,128)}), f32[256,768]{1,0:T(8,128)}) %all-reduce.2.cloned.1.call-update) | async-done | bytes 786448 | tf_op jit(solution)/shard_map/psum | solution.py:62
  638.9 2.1 broadcast_multiply_fusion
  (7 shorter events, 0.1 us)
Async XLA Ops:
  7.2 7.8 %copy-start = (bf16[1280,768]{1,0:T(8,128)(2,1)S(1)}, bf16[1280,768]{1,0:T(8,128)(2,1)}, u32[]{:S(2)}) copy-start(bf16[1280,768]{1,0:T(8,128)(2,1)} %param.5) | copy-start | bytes 5898244
  7.2 14.1 %all-to-all-start = ((s32[16,1,128]{2,1,0:T(1,128)}), s32[16,1,128]{2,1,0:T(1,128)S(1)}, u32[]{:S(2)}, u32[]{:S(2)}) async-start(s32[16,1,128]{2,1,0:T(1,128)} %bitcast.29), calls=%async_computation | async-start | bytes 16384 | tf_op jit(solution)/shard_map/all_to_all | solution.py:41
  30.3 4.5 copy-start.1
  30.3 16.8 %all-to-all-start.1 = ((bf16[16,128,256]{2,1,0:T(8,128)(2,1)}), bf16[16,128,256]{2,1,0:T(8,128)(2,1)}, u32[]{:S(2)}, u32[]{:S(2)}) async-start(bf16[16,128,256]{2,1,0:T(8,128)(2,1)} %bitcast.20), calls=%async_computation.1 | async-start | bytes 2097152 | tf_op jit(solution)/shard_map/all_to_all | solution.py:44
  78.2 2.5 copy-start.2
  131.9 16.3 %all-to-all-start.2 = ((bf16[16,128,256]{2,1,0:T(8,128)(2,1)}), bf16[16,128,256]{2,1,0:T(8,128)(2,1)}, u32[]{:S(2)}, u32[]{:S(2)}) async-start(bf16[16,128,256]{2,1,0:T(8,128)(2,1)} %bitcast.10), calls=%async_computation.2 | async-start | bytes 2097152 | tf_op jit(solution)/shard_map/all_to_all | solution.py:48
  136.2 502.6 %all-reduce.2.cloned.1.call-start = ((), (), s32[]{:S(2)}) async-start(), calls=%async_computation.3 | async-start | bytes 1572864 | tf_op jit(solution)/shard_map/psum | solution.py:62
Sparse Core Ops, SparseCore 0:
  163.3 475.4 all-reduce.1
where the time goes:
time: 649 us; the launch traced here: 648 us
  waiting for transfers between devices  500 us (77%)
  other arithmetic  69 us (11%)
  local copies, waits for them, and re-layouts  41.7 us (6%)
  starting transfers between devices  16.6 us (3%)
  between operations  14.2 us (2%)
    psum x1, waiting for transfers between devices, local(): weight_total = lax.psum(partial_value, ('group', 'dev'))  473 us
    scatter-add x1, other arithmetic, triplet_gradients(): gradient = gradient.at[triple[1]].add(-pull_term)  16.7 us
    scatter-add x1, other arithmetic, triplet_gradients(): gradient = gradient.at[triple[2]].add(push_term)  16.6 us
    scatter-add x1, other arithmetic, triplet_gradients(): gradient = gradient.at[triple[0]].add(pull_term - push_term)  15.1 us
    scatter-add x1, other arithmetic, local(): row_total = gradient[:shard_rows].at[served_index.reshape(-1)].add(return...  13.4 us
  transfers between devices with their start and end apart: 4, of which 4 were waited for; matrix products, arithmetic and copies ran while one was open for 1% of the time, Pallas kernels for 0%

commit v1 on v0

v1 whole, which is shorter than its diff:
```python
import functools
import math

import jax
import jax.numpy as jnp
from jax import lax
from jax.experimental import pallas as pl
from jax.experimental.pallas import tpu as pltpu
from jax.sharding import PartitionSpec as P

distance_scale = 0.0625
margin = 1.0
pull_share = 0.5
BF = jnp.bfloat16
F32 = jnp.float32
BLOCK = 256
LANES = 128
NT = (((1,), (1,)), ((), ()))
NN = (((1,), (0,)), ((), ()))
PARAMS = pltpu.CompilerParams(vmem_limit_bytes=56 * 1024 * 1024)


def row_numbers():
    return lax.broadcasted_iota(jnp.int32, (BLOCK, LANES), 0).astype(F32).astype(BF)


def hits(index, base, numbers):
    place = (index - base).astype(F32).astype(BF)
    return [
        jnp.broadcast_to(place[:, c : c + LANES], (BLOCK, LANES)) == numbers
        for c in range(0, index.shape[1], LANES)
    ]


def select(mask, value):
    return jnp.where(mask, jnp.full((BLOCK, LANES), value, BF), jnp.zeros((BLOCK, LANES), BF))


def one_hot(index, base, rows, numbers, value=1.0):
    blocks = []
    for r in range(0, rows, BLOCK):
        blocks.append(
            jnp.concatenate([select(m, value) for m in hits(index, base + r, numbers)], axis=1)
        )
    return blocks[0] if len(blocks) == 1 else jnp.concatenate(blocks, axis=0)


def difference(anchor, other, rows, numbers):
    blocks = []
    for r in range(0, rows, BLOCK):
        pieces = [
            select(m, 1.0) - select(n, 1.0)
            for m, n in zip(hits(anchor, r, numbers), hits(other, r, numbers))
        ]
        blocks.append(jnp.concatenate(pieces, axis=1))
    return jnp.concatenate(blocks, axis=0)


def dot(a, b, contract=NN):
    return lax.dot_general(a, b, contract, preferred_element_type=F32)


def project_kernel(embeddings_ref, projection_ref, out_ref):
    out_ref[...] = dot(projection_ref[...], embeddings_ref[...], NT).astype(BF)


def serve_kernel(table_ref, wanted_ref, out_ref):
    numbers = row_numbers()
    groups, rank, slots = out_ref.shape
    step = 4

    def body(i, carry):
        first = i * step
        index = jnp.concatenate([wanted_ref[first + j] for j in range(step)], axis=1)
        served = dot(table_ref[...], one_hot(index, 0, table_ref.shape[1], numbers)).astype(BF)
        for j in range(step):
            out_ref[first + j] = served[:, j * slots : (j + 1) * slots]
        return carry

    lax.fori_loop(0, groups // step, body, 0)


def own_gather_kernel(table_ref, triplets_ref, positive_ref, negative_ref):
    numbers = row_numbers()
    rows = table_ref.shape[1]
    step = 512

    def body(i, carry):
        at = pl.ds(pl.multiple_of(i * step, step), step)
        anchor = triplets_ref[0:1, at]
        positive_ref[:, at] = dot(table_ref[...], difference(anchor, triplets_ref[1:2, at], rows, numbers))
        negative_ref[:, at] = dot(table_ref[...], difference(anchor, triplets_ref[2:3, at], rows, numbers))
        return carry

    lax.fori_loop(0, triplets_ref.shape[1] // step, body, 0)


def middle_kernel(fetched_ref, triplets_ref, cotangent_ref, positive_ref, negative_ref,
                  remote_ref, pull_ref, push_ref, table_ref, *, own):
    numbers = row_numbers()
    groups, rank, slots = fetched_ref.shape
    rows = groups * slots
    step = 512
    for g in range(groups):
        table_ref[:, g * slots : (g + 1) * slots] = fetched_ref[g]

    def gather(i, carry):
        at = pl.ds(pl.multiple_of(i * step, step), step)
        to_positive = positive_ref[:, at] - dot(
            table_ref[...], one_hot(triplets_ref[1:2, at], own, rows, numbers))
        to_negative = negative_ref[:, at] - dot(
            table_ref[...], one_hot(triplets_ref[2:3, at], own, rows, numbers))
        near = distance_scale * jnp.sum(to_positive * to_positive, axis=0, keepdims=True)
        far = distance_scale * jnp.sum(to_negative * to_negative, axis=0, keepdims=True)
        gate = jax.nn.sigmoid(margin + near - far)
        weight = cotangent_ref[:, at]
        pull = 2.0 * distance_scale * weight * (1.0 - pull_share + pull_share * gate)
        push = 2.0 * distance_scale * weight * pull_share * gate
        pull_ref[:, at] = (-pull * to_positive).astype(BF)
        push_ref[:, at] = (push * to_negative).astype(BF)
        return carry

    lax.fori_loop(0, triplets_ref.shape[1] // step, gather, 0)
    per = BLOCK // slots

    def scatter(i, carry):
        base = own + i * BLOCK
        total = dot(pull_ref[...], one_hot(triplets_ref[1:2, :], base, BLOCK, numbers), NT)
        total = total + dot(push_ref[...], one_hot(triplets_ref[2:3, :], base, BLOCK, numbers), NT)
        total = total.astype(BF)
        for j in range(per):
            remote_ref[i * per + j] = total[:, j * slots : (j + 1) * slots]
        return carry

    lax.fori_loop(0, rows // BLOCK, scatter, 0)


def own_scatter_kernel(pull_ref, push_ref, triplets_ref, out_ref):
    numbers = row_numbers()

    def body(i, carry):
        base = i * BLOCK
        anchor = hits(triplets_ref[0:1, :], base, numbers)
        parts = []
        for row in (1, 2):
            other = hits(triplets_ref[row : row + 1, :], base, numbers)
            parts.append(jnp.concatenate(
                [select(n, 1.0) - select(m, 1.0) for m, n in zip(anchor, other)], axis=1))
        total = dot(pull_ref[...], parts[0], NT) + dot(push_ref[...], parts[1], NT)
        out_ref[:, pl.ds(pl.multiple_of(base, BLOCK), BLOCK)] = total
        return carry

    lax.fori_loop(0, out_ref.shape[1] // BLOCK, body, 0)


def finish_kernel(own_ref, returned_ref, wanted_ref, embeddings_ref, rounded_ref, partial_ref, back_ref):
    numbers = row_numbers()
    groups, rank, slots = returned_ref.shape
    for g in range(groups):
        back_ref[:, g * slots : (g + 1) * slots] = returned_ref[g]
    index = jnp.concatenate([wanted_ref[g] for g in range(groups)], axis=1)

    def body(i, carry):
        at = pl.ds(pl.multiple_of(i * BLOCK, BLOCK), BLOCK)
        total = own_ref[:, at] + dot(back_ref[...], one_hot(index, i * BLOCK, BLOCK, numbers), NT)
        rounded_ref[:, at] = total.astype(BF)
        return carry

    lax.fori_loop(0, own_ref.shape[1] // BLOCK, body, 0)
    partial_ref[...] = dot(rounded_ref[...], embeddings_ref[...]).astype(partial_ref.dtype)


def shape(dims, kind):
    return jax.ShapeDtypeStruct(dims, kind)


def exchange(value, axis):
    return lax.all_to_all(value, axis, split_axis=0, concat_axis=0, tiled=True)


def reduce_all(partial, factor):
    groups, members = lax.axis_size("group"), lax.axis_size("dev")
    rank, width = partial.shape
    mine = exchange(partial.reshape(groups, rank // groups, width), "group")
    mine = jnp.sum(mine.astype(F32), axis=0)
    mine = mine.reshape(members, -1)
    mine = jnp.sum(exchange(mine, "dev"), axis=0) * factor
    mine = exchange(jnp.broadcast_to(mine[None], (members,) + mine.shape), "dev")
    mine = mine.reshape(rank // groups, width)
    whole = exchange(jnp.broadcast_to(mine[None], (groups,) + mine.shape), "group")
    return whole.reshape(rank, width)


def local(embeddings, projection, triplets, cotangent, wanted_rows):
    rows, width = embeddings.shape
    rank = projection.shape[0]
    count = triplets.shape[1]
    groups, slots = wanted_rows.shape
    wanted = exchange(wanted_rows.reshape(groups, 1, slots), "group")
    table = pl.pallas_call(project_kernel, out_shape=shape((rank, rows), BF),
                           compiler_params=PARAMS, name="project")(embeddings, projection)
    served = pl.pallas_call(serve_kernel, out_shape=shape((groups, rank, slots), BF),
                            compiler_params=PARAMS, name="serve")(table, wanted)
    fetched = exchange(served, "group")
    positive, negative = pl.pallas_call(
        own_gather_kernel, out_shape=[shape((rank, count), F32)] * 2,
        compiler_params=PARAMS, name="own_gather")(table, triplets)
    remote, pull, push = pl.pallas_call(
        functools.partial(middle_kernel, own=rows),
        out_shape=[shape((groups, rank, slots), BF), shape((rank, count), BF), shape((rank, count), BF)],
        scratch_shapes=[pltpu.VMEM((rank, groups * slots), BF)],
        compiler_params=PARAMS, name="middle",
    )(fetched, triplets, cotangent.reshape(1, count), positive, negative)
    returned = exchange(remote, "group")
    own = pl.pallas_call(own_scatter_kernel, out_shape=shape((rank, rows), F32),
                         compiler_params=PARAMS, name="own_scatter")(pull, push, triplets)
    rounded, partial = pl.pallas_call(
        finish_kernel,
        out_shape=[shape((rank, rows), BF), shape((rank, width), BF)],
        scratch_shapes=[pltpu.VMEM((rank, groups * slots), BF)],
        compiler_params=PARAMS, name="finish",
    )(own, returned, wanted, embeddings)
    factor = 1.0 / math.sqrt(cotangent.shape[0] * groups * lax.axis_size("dev"))
    weight_grad = reduce_all(partial, factor)
    row_grad = lax.dot_general(rounded, projection, (((0,), (0,)), ((), ())),
                               preferred_element_type=F32).astype(BF)
    return (row_grad, weight_grad)


def solution(mesh):
    return jax.shard_map(
        local,
        mesh=mesh,
        in_specs=(
            P(("group", "dev"), None),
            P(),
            P(None, ("group", "dev")),
            P(("group", "dev")),
            P(("group", "dev"), None),
        ),
        out_specs=(P(("group", "dev"), None), P()),
        check_vma=False,
    )
```

time: 649 us -> 161 us (0.25)
  waiting for transfers between devices: 500 us -> 25.5 us
  other arithmetic: 69 us -> 0.24 us
  blocking collectives: 0 us -> 66 us
  Pallas kernels: 0 us -> 41.8 us
  local copies, waits for them, and re-layouts: 41.7 us -> 4.47 us
  between operations: 14.2 us -> 0.71 us
    psum x1 -> x0, waiting for transfers between devices: 473 us -> none  [local(): weight_total = lax.psum(partial_value, ('group', 'dev'))]
    all_to_all x0 -> x3, blocking collectives: none -> 66 us  [exchange(): return lax.all_to_all(value, axis, split_axis=0, concat_axis=0, tiled=True)]
    scatter-add x4 -> x0, other arithmetic: 61.9 us -> none  [the longest x1 16.7 us: triplet_gradients(): gradient = gradient.at[triple[1]].add(-pull_term)]
    pallas_call x0 -> x6, Pallas kernels: none -> 41.8 us  [the longest x1 15.5 us: local(): pl.pallas_call(functools.partial(middle_kernel, own=rows), out_shape=[sha...]
    gather x4 -> x0, local copies, waits for them, and re-layouts: 37.6 us -> none  [the longest x1 10.1 us: triplet_gradients(): negative_rows = lookup[triple[2]].astype(jnp.float32)]
    all_to_all x3 -> x4, starting transfers between devices: 16.6 us -> 19.2 us  [exchange(): return lax.all_to_all(value, axis, split_axis=0, concat_axis=0, tiled=True)]
    all_to_all x3 -> x4, waiting for transfers between devices: 27.3 us -> 25.5 us  [exchange(): return lax.all_to_all(value, axis, split_axis=0, concat_axis=0, tiled=True)]
  transfers between devices with their start and end apart: 4 -> 4, of which waited for: 4 -> 4; matrix products, arithmetic and copies ran while one was open for 1% -> 1% of each run, Pallas kernels for 0% -> 10%
where the time goes in v1:
time: 161 us; the launch traced here: 160 us
  blocking collectives  66 us (41%)
  Pallas kernels  41.8 us (26%)
  waiting for transfers between devices  25.5 us (16%)
  starting transfers between devices  19.2 us (12%)
  local copies, waits for them, and re-layouts  4.47 us (3%)
  matrix products  2 us (1%)
    all_to_all x3, blocking collectives, exchange(): return lax.all_to_all(value, axis, split_axis=0, concat_axis=0, tiled=True)  66 us
    all_to_all x4, waiting for transfers between devices, exchange(): return lax.all_to_all(value, axis, split_axis=0, concat_axis=0, tiled=True)  25.5 us
    all_to_all x4, starting transfers between devices, exchange(): return lax.all_to_all(value, axis, split_axis=0, concat_axis=0, tiled=True)  19.2 us
    pallas_call x1, Pallas kernels, local(): pl.pallas_call(functools.partial(middle_kernel, own=rows), out_shape=[sha...  15.5 us
    pallas_call x1, Pallas kernels, local(): pl.pallas_call(finish_kernel, out_shape=[shape((rank, rows), BF), shape((...  6.44 us
    pallas_call x1, Pallas kernels, local(): pl.pallas_call(own_scatter_kernel, out_shape=shape((rank, rows), F32), co...  6.4 us
    pallas_call x1, Pallas kernels, local(): pl.pallas_call(own_gather_kernel, out_shape=[shape((rank, count), F32)] *...  6.25 us
    pallas_call x1, Pallas kernels, local(): pl.pallas_call(serve_kernel, out_shape=shape((groups, rank, slots), BF),...  4.12 us
  transfers between devices with their start and end apart: 4, of which 4 were waited for; matrix products, arithmetic and copies ran while one was open for 1% of the time, Pallas kernels for 10%

profile of v1, /device:TPU:1, one launch (start us, length us, event | category | flops | bytes accessed | tf_op | source)
XLA Modules:
  0.0 159.9 jit_solution(7991593656931172612)
XLA Ops:
  0.6 7.6 %all-to-all-start = ((s32[16,1,128]{2,1,0:T(1,128)}), s32[16,1,128]{2,1,0:T(1,128)S(1)}, u32[]{:S(2)}, u32[]{:S(2)}) async-start(s32[16,1,128]{2,1,0:T(1,128)} %bitcast.9), calls=%async_computation | async-start | bytes 16384 | tf_op jit(solution)/shard_map/all_to_all | solution.py:178
  8.2 3.1 %project.1.table_ref = bf16[256,1280]{1,0:T(8,128)(2,1)} custom-call(bf16[1280,768]{1,0:T(8,128)(2,1)} %embeddings_ref.3, bf16[256,768]{1,0:T(8,128)(2,1)} %projection_ref.1), custom_call_target="tpu_custom_call" | custom-call | tf_op jit(solution)/shard_map/project/pallas_call | solution.py:200
  11.4 3.2 %all-to-all-done.wanted_ref = s32[16,1,128]{2,1,0:T(1,128)S(1)} async-done(((s32[16,1,128]{2,1,0:T(1,128)}), s32[16,1,128]{2,1,0:T(1,128)S(1)}, u32[]{:S(2)}, u32[]{:S(2)}) %all-to-all-start) | async-done | bytes 8224 | tf_op jit(solution)/shard_map/all_to_all | solution.py:178
  14.6 0.0 copy-start.4
  14.6 0.6 copy-done.4
  15.2 4.1 %serve.1 = bf16[16,256,128]{2,1,0:T(8,128)(2,1)} custom-call(bf16[256,1280]{1,0:T(8,128)(2,1)} %project.1.table_ref, s32[16,1,128]{2,1,0:T(1,128)} %copy-done.4), custom_call_target="tpu_custom_call" | custom-call | tf_op jit(solution)/shard_map/serve/pallas_call | solution.py:202
  19.3 3.7 %all-to-all-start.1 = ((bf16[16,256,128]{2,1,0:T(8,128)(2,1)}), bf16[16,256,128]{2,1,0:T(8,128)(2,1)S(1)}, u32[]{:S(2)}, u32[]{:S(2)}) async-start(bf16[16,256,128]{2,1,0:T(8,128)(2,1)} %serve.1), calls=%async_computation.1 | async-start | bytes 2097152 | tf_op jit(solution)/shard_map/all_to_all | solution.py:178
  22.9 6.2 %own_gather.1 = (f32[256,2048]{1,0:T(8,128)}, f32[256,2048]{1,0:T(8,128)}) custom-call(bf16[256,1280]{1,0:T(8,128)(2,1)} %project.1.table_ref, s32[3,2048]{1,0:T(4,128)} %triplets_ref.5), custom_call_target="tpu_custom_call" | custom-call | tf_op jit(solution)/shard_map/own_gather/pallas_call | solution.py:205
  29.2 6.0 %all-to-all-done.1.fetched_ref = bf16[16,256,128]{2,1,0:T(8,128)(2,1)S(1)} async-done(((bf16[16,256,128]{2,1,0:T(8,128)(2,1)}), bf16[16,256,128]{2,1,0:T(8,128)(2,1)S(1)}, u32[]{:S(2)}, u32[]{:S(2)}) %all-to-all-start.1) | async-done | bytes 1048608 | tf_op jit(solution)/shard_map/all_to_all | solution.py:178
  35.2 0.0 copy-start
  35.2 1.0 copy-done
  36.2 15.5 %middle.1 = (bf16[16,256,128]{2,1,0:T(8,128)(2,1)}, bf16[256,2048]{1,0:T(8,128)(2,1)}, bf16[256,2048]{1,0:T(8,128)(2,1)}) custom-call(bf16[16,256,128]{2,1,0:T(8,128)(2,1)} %copy-done, s32[3,2048]{1,0:T(4,128)} %triplets_ref.5, f32[1,2048]{1,0:T(1,128)} %bitcast.8, f32[256,2048]{1,0:T(8,128)} %get-tuple-element.9.positive_ref, ...), custom_call_target="tpu_custom_call" | custom-call | tf_op jit(solution)/shard_map/middle/pallas_call | solution.py:208
  51.7 4.3 %all-to-all-start.2 = ((bf16[16,256,128]{2,1,0:T(8,128)(2,1)}), bf16[16,256,128]{2,1,0:T(8,128)(2,1)S(1)}, u32[]{:S(2)}, u32[]{:S(2)}) async-start(bf16[16,256,128]{2,1,0:T(8,128)(2,1)} %get-tuple-element.13), calls=%async_computation.2 | async-start | bytes 2097152 | tf_op jit(solution)/shard_map/all_to_all | solution.py:178
  56.0 6.4 %own_scatter.1.own_ref = f32[256,1280]{1,0:T(8,128)} custom-call(bf16[256,2048]{1,0:T(8,128)(2,1)} %get-tuple-element.11.pull_ref, bf16[256,2048]{1,0:T(8,128)(2,1)} %get-tuple-element.12.push_ref, s32[3,2048]{1,0:T(4,128)} %triplets_ref.5), custom_call_target="tpu_custom_call" | custom-call | tf_op jit(solution)/shard_map/own_scatter/pallas_call | solution.py:215
  62.4 5.4 %all-to-all-done.2.returned_ref = bf16[16,256,128]{2,1,0:T(8,128)(2,1)S(1)} async-done(((bf16[16,256,128]{2,1,0:T(8,128)(2,1)}), bf16[16,256,128]{2,1,0:T(8,128)(2,1)S(1)}, u32[]{:S(2)}, u32[]{:S(2)}) %all-to-all-start.2) | async-done | bytes 1048608 | tf_op jit(solution)/shard_map/all_to_all | solution.py:178
  67.8 0.0 copy-start.1
  67.8 1.0 copy-done.1
  68.8 6.4 %finish.1 = (bf16[256,1280]{1,0:T(8,128)(2,1)}, bf16[256,768]{1,0:T(8,128)(2,1)}) custom-call(f32[256,1280]{1,0:T(8,128)} %own_scatter.1.own_ref, bf16[16,256,128]{2,1,0:T(8,128)(2,1)} %copy-done.1, s32[16,1,128]{2,1,0:T(1,128)} %copy-done.4, bf16[1280,768]{1,0:T(8,128)(2,1)} %embeddings_ref.3), custom_call_target="tpu_custom_call" | custom-call | tf_op jit(solution)/shard_map/finish/pallas_call | solution.py:217
  75.3 0.0 copy-start.2
  75.3 0.0 copy-start.3
  75.3 11.7 %all_to_all.40 = bf16[16,16,768]{2,1,0:T(8,128)(2,1)S(1)} all-to-all(bf16[16,16,768]{2,1,0:T(8,128)(2,1)} %bitcast.7), channel_id=1, replica_groups=mesh['group'=16,'dev'=32] {'group'}, dimensions={0} | all-to-all | bytes 786432 | tf_op jit(solution)/shard_map/all_to_all | solution.py:178
  87.0 0.1 convert_reduce_fusion
  87.0 0.1 all_to_all.29
  87.1 37.5 %all_to_all.41 = f32[32,1,384]{2,1,0:T(1,128)S(1)} all-to-all(f32[32,1,384]{2,1,0:T(1,128)S(1)} %all_to_all.29), channel_id=1, replica_groups=mesh['group'=16,'dev'=32] {'dev'}, dimensions={0} | all-to-all | bytes 98304 | tf_op jit(solution)/shard_map/all_to_all | solution.py:178
  124.6 0.1 reduce_sum.19
  124.7 16.8 %all_to_all.42 = f32[32,1,384]{2,1,0:T(1,128)S(1)} all-to-all(f32[32,1,384]{2,1,0:T(1,128)S(1)} %broadcast_in_dim.6), channel_id=1, replica_groups=mesh['group'=16,'dev'=32] {'dev'}, dimensions={0} | all-to-all | bytes 98304 | tf_op jit(solution)/shard_map/all_to_all | solution.py:178
  141.5 0.1 reduce.1
  141.6 1.0 broadcast_in_dim.15
  142.6 3.6 %all-to-all-start.6 = ((f32[16,16,768]{2,1,0:T(8,128)}), f32[16,16,768]{2,1,0:T(8,128)S(1)}, u32[]{:S(2)}, u32[]{:S(2)}) async-start(f32[16,16,768]{2,1,0:T(8,128)} %broadcast_in_dim.15), calls=%async_computation.6 | async-start | bytes 1572864 | tf_op jit(solution)/shard_map/all_to_all | solution.py:178
  146.2 0.0 copy-done.2
  146.2 0.0 copy-done.3
  146.2 2.0 %convolution_convert_fusion = bf16[1280,768]{1,0:T(8,128)(2,1)} fusion(bf16[256,1280]{1,0:T(8,128)(2,1)S(1)} %copy-done.3, bf16[256,768]{1,0:T(8,128)(2,1)S(1)} %copy-done.2), kind=kOutput, calls=%fused_computation | convolution fusion | flops 504299520 | bytes 3014656 | tf_op jit(solution)/shard_map/dot_general | solution.py:225
  148.2 10.8 %all-to-all-done.6 = f32[16,16,768]{2,1,0:T(8,128)S(1)} async-done(((f32[16,16,768]{2,1,0:T(8,128)}), f32[16,16,768]{2,1,0:T(8,128)S(1)}, u32[]{:S(2)}, u32[]{:S(2)}) %all-to-all-start.6) | async-done | bytes 786464 | tf_op jit(solution)/shard_map/all_to_all | solution.py:178
  159.0 0.9 copy.8
  (3 shorter events, 0.1 us)
Async XLA Ops:
  0.6 13.9 %all-to-all-start = ((s32[16,1,128]{2,1,0:T(1,128)}), s32[16,1,128]{2,1,0:T(1,128)S(1)}, u32[]{:S(2)}, u32[]{:S(2)}) async-start(s32[16,1,128]{2,1,0:T(1,128)} %bitcast.9), calls=%async_computation | async-start | bytes 16384 | tf_op jit(solution)/shard_map/all_to_all | solution.py:178
  14.6 0.6 copy-start.4
  19.3 16.0 %all-to-all-start.1 = ((bf16[16,256,128]{2,1,0:T(8,128)(2,1)}), bf16[16,256,128]{2,1,0:T(8,128)(2,1)S(1)}, u32[]{:S(2)}, u32[]{:S(2)}) async-start(bf16[16,256,128]{2,1,0:T(8,128)(2,1)} %serve.1), calls=%async_computation.1 | async-start | bytes 2097152 | tf_op jit(solution)/shard_map/all_to_all | solution.py:178
  35.2 1.0 copy-start
  51.7 16.2 %all-to-all-start.2 = ((bf16[16,256,128]{2,1,0:T(8,128)(2,1)}), bf16[16,256,128]{2,1,0:T(8,128)(2,1)S(1)}, u32[]{:S(2)}, u32[]{:S(2)}) async-start(bf16[16,256,128]{2,1,0:T(8,128)(2,1)} %get-tuple-element.13), calls=%async_computation.2 | async-start | bytes 2097152 | tf_op jit(solution)/shard_map/all_to_all | solution.py:178
  67.8 1.0 copy-start.1
  75.3 70.9 %copy-start.2 = (bf16[256,768]{1,0:T(8,128)(2,1)S(1)}, bf16[256,768]{1,0:T(8,128)(2,1)}, u32[]{:S(2)}) copy-start(bf16[256,768]{1,0:T(8,128)(2,1)} %projection_ref.1) | copy-start | bytes 1179652
  75.3 71.0 %copy-start.3 = (bf16[256,1280]{1,0:T(8,128)(2,1)S(1)}, bf16[256,1280]{1,0:T(8,128)(2,1)}, u32[]{:S(2)}) copy-start(bf16[256,1280]{1,0:T(8,128)(2,1)} %get-tuple-element.14) | copy-start | bytes 1966084
  142.6 16.4 %all-to-all-start.6 = ((f32[16,16,768]{2,1,0:T(8,128)}), f32[16,16,768]{2,1,0:T(8,128)S(1)}, u32[]{:S(2)}, u32[]{:S(2)}) async-start(f32[16,16,768]{2,1,0:T(8,128)} %broadcast_in_dim.15), calls=%async_computation.6 | async-start | bytes 1572864 | tf_op jit(solution)/shard_map/all_to_all | solution.py:178

commit v2 on v1

v2 whole, which is shorter than its diff:
```python
import functools
import math

import jax
import jax.numpy as jnp
from jax import lax
from jax.experimental import pallas as pl
from jax.experimental.pallas import tpu as pltpu
from jax.sharding import PartitionSpec as P

distance_scale = 0.0625
margin = 1.0
pull_share = 0.5
BF = jnp.bfloat16
F32 = jnp.float32
BLOCK = 256
LANES = 128
NT = (((1,), (1,)), ((), ()))
NN = (((1,), (0,)), ((), ()))
PARAMS = pltpu.CompilerParams(vmem_limit_bytes=24 * 1024 * 1024)


def row_numbers():
    return lax.broadcasted_iota(jnp.int32, (BLOCK, LANES), 0).astype(F32).astype(BF)


def hits(index, base, numbers):
    place = (index - base).astype(F32).astype(BF)
    return [
        jnp.broadcast_to(place[:, c : c + LANES], (BLOCK, LANES)) == numbers
        for c in range(0, index.shape[1], LANES)
    ]


def select(mask, value):
    return jnp.where(mask, jnp.full((BLOCK, LANES), value, BF), jnp.zeros((BLOCK, LANES), BF))


def one_hot(index, base, rows, numbers, value=1.0):
    blocks = []
    for r in range(0, rows, BLOCK):
        blocks.append(
            jnp.concatenate([select(m, value) for m in hits(index, base + r, numbers)], axis=1)
        )
    return blocks[0] if len(blocks) == 1 else jnp.concatenate(blocks, axis=0)


def difference(anchor, other, rows, numbers):
    blocks = []
    for r in range(0, rows, BLOCK):
        pieces = [
            select(m, 1.0) - select(n, 1.0)
            for m, n in zip(hits(anchor, r, numbers), hits(other, r, numbers))
        ]
        blocks.append(jnp.concatenate(pieces, axis=1))
    return jnp.concatenate(blocks, axis=0)


def dot(a, b, contract=NN):
    return lax.dot_general(a, b, contract, preferred_element_type=F32)


def project_kernel(embeddings_ref, projection_ref, out_ref):
    out_ref[...] = dot(projection_ref[...], embeddings_ref[...], NT).astype(BF)


def serve_kernel(table_ref, wanted_ref, out_ref):
    numbers = row_numbers()
    groups, rank, slots = out_ref.shape
    step = 4
    for first in range(0, groups, step):
        index = jnp.concatenate([wanted_ref[first + j] for j in range(step)], axis=1)
        served = dot(table_ref[...], one_hot(index, 0, table_ref.shape[1], numbers)).astype(BF)
        for j in range(step):
            out_ref[first + j] = served[:, j * slots : (j + 1) * slots]


def own_gather_kernel(table_ref, triplets_ref, positive_ref, negative_ref):
    numbers = row_numbers()
    rows = table_ref.shape[1]
    step = 512
    for i in range(0, triplets_ref.shape[1], step):
        at = pl.ds(i, step)
        anchor = triplets_ref[0:1, at]
        positive_ref[:, at] = dot(table_ref[...], difference(anchor, triplets_ref[1:2, at], rows, numbers))
        negative_ref[:, at] = dot(table_ref[...], difference(anchor, triplets_ref[2:3, at], rows, numbers))


def middle_kernel(fetched_ref, triplets_ref, cotangent_ref, positive_hbm, negative_hbm,
                  remote_ref, pull_hbm, push_hbm,
                  table_ref, positive_ref, negative_ref, pull_ref, push_ref, arrived, left, *, own):
    incoming = [pltpu.make_async_copy(positive_hbm, positive_ref, arrived.at[0]),
                pltpu.make_async_copy(negative_hbm, negative_ref, arrived.at[1])]
    outgoing = [pltpu.make_async_copy(pull_ref, pull_hbm, left.at[0]),
                pltpu.make_async_copy(push_ref, push_hbm, left.at[1])]
    for copy in incoming:
        copy.start()
    numbers = row_numbers()
    groups, rank, slots = fetched_ref.shape
    rows = groups * slots
    step = 512
    for g in range(groups):
        table_ref[:, g * slots : (g + 1) * slots] = fetched_ref[g]
    for i in range(0, triplets_ref.shape[1], step):
        at = pl.ds(i, step)
        positive = dot(table_ref[...], one_hot(triplets_ref[1:2, at], own, rows, numbers))
        negative = dot(table_ref[...], one_hot(triplets_ref[2:3, at], own, rows, numbers))
        if i == 0:
            for copy in incoming:
                copy.wait()
        to_positive = positive_ref[:, at] - positive
        to_negative = negative_ref[:, at] - negative
        near = distance_scale * jnp.sum(to_positive * to_positive, axis=0, keepdims=True)
        far = distance_scale * jnp.sum(to_negative * to_negative, axis=0, keepdims=True)
        gate = jax.nn.sigmoid(margin + near - far)
        weight = cotangent_ref[:, at]
        pull = 2.0 * distance_scale * weight * (1.0 - pull_share + pull_share * gate)
        push = 2.0 * distance_scale * weight * pull_share * gate
        pull_ref[:, at] = (-pull * to_positive).astype(BF)
        push_ref[:, at] = (push * to_negative).astype(BF)
    for copy in outgoing:
        copy.start()
    per = step // slots
    for i in range(rows // step):
        base = own + i * step
        total = dot(pull_ref[...], one_hot(triplets_ref[1:2, :], base, step, numbers), NT)
        total = total + dot(push_ref[...], one_hot(triplets_ref[2:3, :], base, step, numbers), NT)
        total = total.astype(BF)
        for j in range(per):
            remote_ref[i * per + j] = total[:, j * slots : (j + 1) * slots]
    for copy in outgoing:
        copy.wait()


def own_scatter_kernel(pull_ref, push_ref, triplets_ref, out_ref):
    numbers = row_numbers()
    for base in range(0, out_ref.shape[1], BLOCK):
        anchor = hits(triplets_ref[0:1, :], base, numbers)
        parts = []
        for row in (1, 2):
            other = hits(triplets_ref[row : row + 1, :], base, numbers)
            parts.append(jnp.concatenate(
                [select(n, 1.0) - select(m, 1.0) for m, n in zip(anchor, other)], axis=1))
        out_ref[:, pl.ds(base, BLOCK)] = dot(pull_ref[...], parts[0], NT) + dot(push_ref[...], parts[1], NT)


def finish_kernel(side_ref, own_hbm, returned_ref, wanted_ref, embeddings_hbm,
                  rounded_ref, kept_ref, sent_ref, back_ref, own_ref, embeddings_ref, arrived):
    own_copy = pltpu.make_async_copy(own_hbm, own_ref, arrived.at[0])
    embeddings_copy = pltpu.make_async_copy(embeddings_hbm, embeddings_ref, arrived.at[1])
    own_copy.start()
    embeddings_copy.start()
    numbers = row_numbers()
    groups, rank, slots = returned_ref.shape
    for g in range(groups):
        back_ref[:, g * slots : (g + 1) * slots] = returned_ref[g]
    index = jnp.concatenate([wanted_ref[g] for g in range(groups)], axis=1)
    for base in range(0, own_ref.shape[1], BLOCK):
        at = pl.ds(base, BLOCK)
        total = dot(back_ref[...], one_hot(index, base, BLOCK, numbers), NT)
        if base == 0:
            own_copy.wait()
        rounded_ref[:, at] = (own_ref[:, at] + total).astype(BF)
    embeddings_copy.wait()
    half = rank // 2
    side = side_ref[0]
    mine = pl.multiple_of(side * half, half)
    theirs = pl.multiple_of((1 - side) * half, half)
    sent_ref[...] = dot(rounded_ref[pl.ds(theirs, half), :], embeddings_ref[...])
    kept_ref[...] = dot(rounded_ref[pl.ds(mine, half), :], embeddings_ref[...])


def pair_kernel(kept_ref, received_ref, out_ref):
    groups, part, width = out_ref.shape
    total = kept_ref[...] + received_ref[...]
    out_ref[...] = total.reshape(groups, part, width).astype(BF)


def spread_kernel(parts_ref, out_ref, *, factor):
    total = parts_ref[0].astype(F32)
    for g in range(1, parts_ref.shape[0]):
        total = total + parts_ref[g].astype(F32)
    total = (total * factor).astype(out_ref.dtype)
    for g in range(out_ref.shape[0]):
        out_ref[g] = total


def join_kernel(side_ref, mine_ref, theirs_ref, out_hbm, left):
    half = mine_ref.shape[0]
    side = side_ref[0]
    copies = []
    for i, (source, start) in enumerate([(mine_ref, side * half), (theirs_ref, (1 - side) * half)]):
        target = out_hbm.at[pl.ds(pl.multiple_of(start, half), half), :]
        copies.append(pltpu.make_async_copy(source, target, left.at[i]))
    for copy in copies:
        copy.start()
    for copy in copies:
        copy.wait()


NEAR, FAR, PLAIN, SCALAR = "near", "far", "plain", "scalar"
SPACES = {NEAR: pltpu.VMEM, FAR: pltpu.HBM, PLAIN: pltpu.HBM}
SPECS = {
    NEAR: pl.BlockSpec(memory_space=pltpu.VMEM),
    FAR: pl.BlockSpec(memory_space=pltpu.HBM),
    PLAIN: pl.BlockSpec(memory_space=pltpu.VMEM),
    SCALAR: pl.BlockSpec(memory_space=pltpu.SMEM),
}


def call(kernel, name, outs, ins, scratch=()):
    args = [a if place == SCALAR else pltpu.with_memory_space_constraint(a, SPACES[place]) for place, a in ins]
    shapes = [SPACES[place](dims, kind) for place, dims, kind in outs]
    result = pl.pallas_call(
        kernel, out_shape=shapes, in_specs=[SPECS[place] for place, _ in ins],
        out_specs=[SPECS[out[0]] for out in outs], scratch_shapes=scratch,
        compiler_params=PARAMS, name=name)(*args)
    return result if len(outs) > 1 else result[0]


def exchange(value, axis, groups=None):
    return lax.all_to_all(value, axis, split_axis=0, concat_axis=0, tiled=True, axis_index_groups=groups)


def local(embeddings, projection, triplets, cotangent, wanted_rows):
    rows, width = embeddings.shape
    rank = projection.shape[0]
    count = triplets.shape[1]
    groups, slots = wanted_rows.shape
    members = lax.axis_size("dev")
    cores = 2
    levels = members // cores
    half = rank // cores
    part = half // groups
    side = (lax.axis_index("dev") & 1).astype(jnp.int32).reshape(1)
    swap = [(i, i ^ 1) for i in range(members)]
    column = [[cores * z + c for z in range(levels)] for c in range(cores)]
    factor = 1.0 / math.sqrt(cotangent.shape[0] * groups * members)
    requests = groups * slots
    two = pltpu.SemaphoreType.DMA((2,))

    wanted = exchange(wanted_rows.reshape(groups, 1, slots), "group")
    table = call(project_kernel, "project", [(NEAR, (rank, rows), BF)],
                 [(NEAR, embeddings), (NEAR, projection)])
    served = call(serve_kernel, "serve", [(NEAR, (groups, rank, slots), BF)], [(NEAR, table), (NEAR, wanted)])
    fetched = exchange(served, "group")
    positive, negative = call(own_gather_kernel, "own_gather", [(PLAIN, (rank, count), F32)] * 2,
                              [(NEAR, table), (NEAR, triplets)])
    remote, pull, push = call(
        functools.partial(middle_kernel, own=rows), "middle",
        [(NEAR, (groups, rank, slots), BF), (FAR, (rank, count), BF), (FAR, (rank, count), BF)],
        [(NEAR, fetched), (NEAR, triplets), (NEAR, cotangent.reshape(1, count)), (FAR, positive), (FAR, negative)],
        [pltpu.VMEM((rank, requests), BF)] + [pltpu.VMEM((rank, count), F32)] * 2
        + [pltpu.VMEM((rank, count), BF)] * 2 + [two, two])
    returned = exchange(remote, "group")
    own = call(own_scatter_kernel, "own_scatter", [(PLAIN, (rank, rows), F32)],
               [(PLAIN, pull), (PLAIN, push), (NEAR, triplets)])
    rounded, kept, sent = call(
        finish_kernel, "finish",
        [(NEAR, (rank, rows), BF), (NEAR, (half, width), F32), (NEAR, (half, width), F32)],
        [(SCALAR, side), (FAR, own), (NEAR, returned), (NEAR, wanted), (FAR, embeddings)],
        [pltpu.VMEM((rank, requests), BF), pltpu.VMEM((rank, rows), F32), pltpu.VMEM((rows, width), BF), two])
    received = lax.ppermute(sent, "dev", swap)
    chip = call(pair_kernel, "pair", [(NEAR, (groups, part, width), BF)], [(NEAR, kept), (NEAR, received)])
    chip = exchange(chip, "group")
    plane = call(functools.partial(spread_kernel, factor=1.0), "plane",
                 [(NEAR, (levels, part, width), BF)], [(NEAR, chip)])
    plane = exchange(plane, "dev", column)
    whole = call(functools.partial(spread_kernel, factor=factor), "whole",
                 [(NEAR, (groups, part, width), F32)], [(NEAR, plane)])
    mine = exchange(whole, "group").reshape(half, width)
    theirs = lax.ppermute(mine, "dev", swap)
    weight_grad = call(join_kernel, "join", [(FAR, (rank, width), F32)],
                       [(SCALAR, side), (NEAR, mine), (NEAR, theirs)], [two])
    row_grad = lax.dot_general(rounded, projection, (((0,), (0,)), ((), ())),
                               preferred_element_type=F32).astype(BF)
    return (row_grad, weight_grad)


def solution(mesh):
    return jax.shard_map(
        local,
        mesh=mesh,
        in_specs=(
            P(("group", "dev"), None),
            P(),
            P(None, ("group", "dev")),
            P(("group", "dev")),
            P(("group", "dev"), None),
        ),
        out_specs=(P(("group", "dev"), None), P()),
        check_vma=False,
    )
```

time: 161 us -> 139 us (0.86)
  blocking collectives: 66 us -> 51.1 us
  starting transfers between devices: 19.2 us -> 32.8 us
  Pallas kernels: 41.8 us -> 30.8 us
  waiting for transfers between devices: 25.5 us -> 18.4 us
  local copies, waits for them, and re-layouts: 4.47 us -> 2.55 us
    ppermute x0 -> x2, starting transfers between devices: none -> 17.1 us  [the longest x1 8.76 us: local(): theirs = lax.ppermute(mine, 'dev', swap)]
    all_to_all x3, blocking collectives: 66 us -> 51.1 us  [exchange(): lax.all_to_all(value, axis, split_axis=0, concat_axis=0, tiled=True, axis...]
    pallas_call x6 -> x10, Pallas kernels: 41.8 us -> 30.8 us  [call(): pl.pallas_call(kernel, out_shape=shapes, in_specs=[SPECS[place] for place...]
    all_to_all x4 -> x3, waiting for transfers between devices: 25.5 us -> 17 us  [exchange(): lax.all_to_all(value, axis, split_axis=0, concat_axis=0, tiled=True, axis...]
    all_to_all x4 -> x3, starting transfers between devices: 19.2 us -> 15.6 us  [exchange(): lax.all_to_all(value, axis, split_axis=0, concat_axis=0, tiled=True, axis...]
    unnamed x11 -> x10, local copies, waits for them, and re-layouts: 3.42 us -> 2.55 us
  transfers between devices with their start and end apart: 4 -> 5, of which waited for: 4 -> 4; matrix products, arithmetic and copies ran while one was open for 1% -> 1% of each run, Pallas kernels for 10% -> 8%
where the time goes in v2:
time: 139 us; the launch traced here: 138 us
  blocking collectives  51.1 us (37%)
  starting transfers between devices  32.8 us (24%)
  Pallas kernels  30.8 us (22%)
  waiting for transfers between devices  18.4 us (13%)
  local copies, waits for them, and re-layouts  2.55 us (2%)
  matrix products  2 us (1%)
    all_to_all x3, blocking collectives, exchange(): lax.all_to_all(value, axis, split_axis=0, concat_axis=0, tiled=True, axis...  51.1 us
    pallas_call x10, Pallas kernels, call(): pl.pallas_call(kernel, out_shape=shapes, in_specs=[SPECS[place] for place...  30.8 us
    all_to_all x3, waiting for transfers between devices, exchange(): lax.all_to_all(value, axis, split_axis=0, concat_axis=0, tiled=True, axis...  17 us
    all_to_all x3, starting transfers between devices, exchange(): lax.all_to_all(value, axis, split_axis=0, concat_axis=0, tiled=True, axis...  15.6 us
    ppermute x1, starting transfers between devices, local(): theirs = lax.ppermute(mine, 'dev', swap)  8.76 us
    ppermute x1, starting transfers between devices, local(): received = lax.ppermute(sent, 'dev', swap)  8.36 us
  transfers between devices with their start and end apart: 5, of which 4 were waited for; matrix products, arithmetic and copies ran while one was open for 1% of the time, Pallas kernels for 8%

profile of v2, /device:TPU:1, one launch (start us, length us, event | category | flops | bytes accessed | tf_op | source)
XLA Modules:
  0.0 138.5 jit_solution(3880469912258463584)
XLA Ops:
  0.6 7.6 %all-to-all-start = ((s32[16,1,128]{2,1,0:T(1,128)}), s32[16,1,128]{2,1,0:T(1,128)S(1)}, u32[]{:S(2)}, u32[]{:S(2)}) async-start(s32[16,1,128]{2,1,0:T(1,128)} %bitcast.9), calls=%async_computation | async-start | bytes 16384 | tf_op jit(solution)/shard_map/all_to_all | solution.py:222
  8.2 0.0 copy-start
  8.2 1.5 %copy-done = bf16[1280,768]{1,0:T(8,128)(2,1)S(1)} copy-done((bf16[1280,768]{1,0:T(8,128)(2,1)S(1)}, bf16[1280,768]{1,0:T(8,128)(2,1)}, u32[]{:S(2)}) %copy-start) | copy-done | bytes 1966104
  9.8 0.0 copy-start.1
  9.8 1.0 copy-done.1
  10.8 0.7 project.1.table_ref
  11.5 0.0 copy-start.3
  11.5 0.0 copy-start.4
  11.5 3.0 %all-to-all-done.wanted_ref = s32[16,1,128]{2,1,0:T(1,128)S(1)} async-done(((s32[16,1,128]{2,1,0:T(1,128)}), s32[16,1,128]{2,1,0:T(1,128)S(1)}, u32[]{:S(2)}, u32[]{:S(2)}) %all-to-all-start) | async-done | bytes 8224 | tf_op jit(solution)/shard_map/all_to_all | solution.py:222
  14.6 2.5 %serve.1 = bf16[16,256,128]{2,1,0:T(8,128)(2,1)} custom-call(bf16[256,1280]{1,0:T(8,128)(2,1)S(1)} %project.1.table_ref, s32[16,1,128]{2,1,0:T(1,128)S(1)} %all-to-all-done.wanted_ref), custom_call_target="tpu_custom_call" | custom-call | tf_op jit(solution)/shard_map/serve/pallas_call | solution.py:214
  17.1 3.7 %all-to-all-start.1 = ((bf16[16,256,128]{2,1,0:T(8,128)(2,1)}), bf16[16,256,128]{2,1,0:T(8,128)(2,1)S(1)}, u32[]{:S(2)}, u32[]{:S(2)}) async-start(bf16[16,256,128]{2,1,0:T(8,128)(2,1)} %serve.1), calls=%async_computation.1 | async-start | bytes 2097152 | tf_op jit(solution)/shard_map/all_to_all | solution.py:222
  20.7 0.0 copy-done.3
  20.7 4.6 %own_gather.1 = (f32[256,2048]{1,0:T(8,128)}, f32[256,2048]{1,0:T(8,128)}) custom-call(bf16[256,1280]{1,0:T(8,128)(2,1)S(1)} %project.1.table_ref, s32[3,2048]{1,0:T(4,128)S(1)} %copy-done.3), custom_call_target="tpu_custom_call" | custom-call | tf_op jit(solution)/shard_map/own_gather/pallas_call | solution.py:214
  25.3 7.6 %all-to-all-done.1.fetched_ref = bf16[16,256,128]{2,1,0:T(8,128)(2,1)S(1)} async-done(((bf16[16,256,128]{2,1,0:T(8,128)(2,1)}), bf16[16,256,128]{2,1,0:T(8,128)(2,1)S(1)}, u32[]{:S(2)}, u32[]{:S(2)}) %all-to-all-start.1) | async-done | bytes 1048608 | tf_op jit(solution)/shard_map/all_to_all | solution.py:222
  33.0 0.0 copy-done.4
  33.0 12.3 %middle.1 = (bf16[16,256,128]{2,1,0:T(8,128)(2,1)}, bf16[256,2048]{1,0:T(8,128)(2,1)}, bf16[256,2048]{1,0:T(8,128)(2,1)}) custom-call(bf16[16,256,128]{2,1,0:T(8,128)(2,1)S(1)} %all-to-all-done.1.fetched_ref, s32[3,2048]{1,0:T(4,128)S(1)} %copy-done.3, f32[1,2048]{1,0:T(1,128)S(1)} %bitcast.8, f32[256,2048]{1,0:T(8,128)} %get-tuple-element.10.positive_hbm, ...), custom_call_target="tpu_custom_call" | custom-call | tf_op jit(solution)/shard_map/middle/pallas_call | solution.py:214
  45.2 4.4 %all-to-all-start.2 = ((bf16[16,256,128]{2,1,0:T(8,128)(2,1)}), bf16[16,256,128]{2,1,0:T(8,128)(2,1)S(1)}, u32[]{:S(2)}, u32[]{:S(2)}) async-start(bf16[16,256,128]{2,1,0:T(8,128)(2,1)} %get-tuple-element.14), calls=%async_computation.2 | async-start | bytes 2097152 | tf_op jit(solution)/shard_map/all_to_all | solution.py:222
  49.6 5.5 %own_scatter.1.own_hbm = f32[256,1280]{1,0:T(8,128)} custom-call(bf16[256,2048]{1,0:T(8,128)(2,1)} %get-tuple-element.12.pull_ref, bf16[256,2048]{1,0:T(8,128)(2,1)} %get-tuple-element.13.push_ref, s32[3,2048]{1,0:T(4,128)S(1)} %copy-done.3), custom_call_target="tpu_custom_call" | custom-call | tf_op jit(solution)/shard_map/own_scatter/pallas_call | solution.py:214
  55.1 6.3 %all-to-all-done.2.returned_ref = bf16[16,256,128]{2,1,0:T(8,128)(2,1)S(1)} async-done(((bf16[16,256,128]{2,1,0:T(8,128)(2,1)}), bf16[16,256,128]{2,1,0:T(8,128)(2,1)S(1)}, u32[]{:S(2)}, u32[]{:S(2)}) %all-to-all-start.2) | async-done | bytes 1048608 | tf_op jit(solution)/shard_map/all_to_all | solution.py:222
  61.5 4.2 %finish.1 = (bf16[256,1280]{1,0:T(8,128)(2,1)S(1)}, f32[128,768]{1,0:T(8,128)S(1)}, f32[128,768]{1,0:T(8,128)S(1)}) custom-call(s32[1]{0:T(128)} %bitcast.side_ref, f32[256,1280]{1,0:T(8,128)} %own_scatter.1.own_hbm, bf16[16,256,128]{2,1,0:T(8,128)(2,1)S(1)} %all-to-all-done.2.returned_ref, s32[16,1,128]{2,1,0:T(1,128)S(1)} %all-to-all-done.wanted_ref, ...), custom_call_target="tpu_custom_call" | custom-call | tf_op jit(solution)/shard_map/finish/pallas_call | solution.py:214
  65.7 0.0 copy-start.2
  65.7 8.4 %collective-permute-start = (f32[128,768]{1,0:T(8,128)S(1)}, f32[128,768]{1,0:T(8,128)S(1)}, u32[]{:S(2)}, u32[]{:S(2)}) collective-permute-start(f32[128,768]{1,0:T(8,128)S(1)} %get-tuple-element.17), channel_id=1, source_target_pairs={{0,1},{1,0},{2,3},{3,2},{4,5},{5,4},{6,7},{7,6},{8,9},{9,8},{10,11... | collective-permute-start | bytes 1179656 | tf_op jit(solution)/shard_map/ppermute | solution.py:263
  74.1 1.3 collective-permute-done.received_ref
  75.5 10.1 %all_to_all.30.parts_ref = bf16[16,8,768]{2,1,0:T(8,128)(2,1)S(1)} all-to-all(bf16[16,8,768]{2,1,0:T(8,128)(2,1)S(1)} %pair.1), channel_id=1, replica_groups=mesh['group'=16,'dev'=32] {'group'}, dimensions={0} | all-to-all | bytes 393216 | tf_op jit(solution)/shard_map/all_to_all | solution.py:222
  85.6 29.6 %all_to_all.31.parts_ref = bf16[16,8,768]{2,1,0:T(8,128)(2,1)S(1)} all-to-all(bf16[16,8,768]{2,1,0:T(8,128)(2,1)S(1)} %plane.1), channel_id=1, replica_groups={{0,2,4,6,8,10,12,14,16,18,20,22,24,26,28,30},{1,3,5,7,9,11,13,15,17,19,..., dimensions={0} | all-to-all | bytes 393216 | tf_op jit(solution)/shard_map/all_to_all | solution.py:222
  115.3 11.4 %all_to_all.32 = f32[16,8,768]{2,1,0:T(8,128)S(1)} all-to-all(f32[16,8,768]{2,1,0:T(8,128)S(1)} %whole.1), channel_id=1, replica_groups=mesh['group'=16,'dev'=32] {'group'}, dimensions={0} | all-to-all | bytes 786432 | tf_op jit(solution)/shard_map/all_to_all | solution.py:222
  126.6 8.8 %collective-permute-start.1 = (f32[128,768]{1,0:T(8,128)S(1)}, f32[128,768]{1,0:T(8,128)S(1)}, u32[]{:S(2)}, u32[]{:S(2)}) collective-permute-start(f32[128,768]{1,0:T(8,128)S(1)} %bitcast.6), channel_id=1, source_target_pairs={{0,1},{1,0},{2,3},{3,2},{4,5},{5,4},{6,7},{7,6},{8,9},{9,8},{10,11... | collective-permute-start | bytes 1179656 | tf_op jit(solution)/shard_map/ppermute | solution.py:272
  135.4 0.0 copy-done.2
  135.4 2.0 %convolution_convert_fusion = bf16[1280,768]{1,0:T(8,128)(2,1)} fusion(bf16[256,1280]{1,0:T(8,128)(2,1)S(1)} %get-tuple-element.15, bf16[256,768]{1,0:T(8,128)(2,1)S(1)} %copy-done.2), kind=kOutput, calls=%fused_computation | convolution fusion | flops 504299520 | bytes 3014656 | tf_op jit(solution)/shard_map/dot_general | solution.py:275
  137.4 0.0 collective-permute-done.1.theirs_ref
  137.4 0.9 join.1
  (3 shorter events, 0.1 us)
Async XLA Ops:
  0.6 13.9 %all-to-all-start = ((s32[16,1,128]{2,1,0:T(1,128)}), s32[16,1,128]{2,1,0:T(1,128)S(1)}, u32[]{:S(2)}, u32[]{:S(2)}) async-start(s32[16,1,128]{2,1,0:T(1,128)} %bitcast.9), calls=%async_computation | async-start | bytes 16384 | tf_op jit(solution)/shard_map/all_to_all | solution.py:222
  8.2 1.5 %copy-start = (bf16[1280,768]{1,0:T(8,128)(2,1)S(1)}, bf16[1280,768]{1,0:T(8,128)(2,1)}, u32[]{:S(2)}) copy-start(bf16[1280,768]{1,0:T(8,128)(2,1)} %embeddings_hbm.1) | copy-start | bytes 5898244
  9.8 1.0 copy-start.1
  11.5 9.2 %copy-start.3 = (s32[3,2048]{1,0:T(4,128)S(1)}, s32[3,2048]{1,0:T(4,128)}, u32[]{:S(2)}) copy-start(s32[3,2048]{1,0:T(4,128)} %triplets_ref.5) | copy-start | bytes 73732
  11.5 21.4 %copy-start.4 = (f32[2048]{0:T(1024)S(1)}, f32[2048]{0:T(1024)}, u32[]{:S(2)}) copy-start(f32[2048]{0:T(1024)} %param.8) | copy-start | bytes 24580
  17.1 15.9 %all-to-all-start.1 = ((bf16[16,256,128]{2,1,0:T(8,128)(2,1)}), bf16[16,256,128]{2,1,0:T(8,128)(2,1)S(1)}, u32[]{:S(2)}, u32[]{:S(2)}) async-start(bf16[16,256,128]{2,1,0:T(8,128)(2,1)} %serve.1), calls=%async_computation.1 | async-start | bytes 2097152 | tf_op jit(solution)/shard_map/all_to_all | solution.py:222
  45.2 16.3 %all-to-all-start.2 = ((bf16[16,256,128]{2,1,0:T(8,128)(2,1)}), bf16[16,256,128]{2,1,0:T(8,128)(2,1)S(1)}, u32[]{:S(2)}, u32[]{:S(2)}) async-start(bf16[16,256,128]{2,1,0:T(8,128)(2,1)} %get-tuple-element.14), calls=%async_computation.2 | async-start | bytes 2097152 | tf_op jit(solution)/shard_map/all_to_all | solution.py:222
  65.7 69.7 %copy-start.2 = (bf16[256,768]{1,0:T(8,128)(2,1)S(1)}, bf16[256,768]{1,0:T(8,128)(2,1)}, u32[]{:S(2)}) copy-start(bf16[256,768]{1,0:T(8,128)(2,1)} %projection_ref.1) | copy-start | bytes 1179652
  65.7 9.7 %collective-permute-start = (f32[128,768]{1,0:T(8,128)S(1)}, f32[128,768]{1,0:T(8,128)S(1)}, u32[]{:S(2)}, u32[]{:S(2)}) collective-permute-start(f32[128,768]{1,0:T(8,128)S(1)} %get-tuple-element.17), channel_id=1, source_target_pairs={{0,1},{1,0},{2,3},{3,2},{4,5},{5,4},{6,7},{7,6},{8,9},{9,8},{10,11... | collective-permute-start | bytes 1179656 | tf_op jit(solution)/shard_map/ppermute | solution.py:263
  126.6 10.8 %collective-permute-start.1 = (f32[128,768]{1,0:T(8,128)S(1)}, f32[128,768]{1,0:T(8,128)S(1)}, u32[]{:S(2)}, u32[]{:S(2)}) collective-permute-start(f32[128,768]{1,0:T(8,128)S(1)} %bitcast.6), channel_id=1, source_target_pairs={{0,1},{1,0},{2,3},{3,2},{4,5},{5,4},{6,7},{7,6},{8,9},{9,8},{10,11... | collective-permute-start | bytes 1179656 | tf_op jit(solution)/shard_map/ppermute | solution.py:272

commit v3 on v2

--- a/solution.py
+++ b/solution.py
@@ -64,15 +64,22 @@
     out_ref[...] = dot(projection_ref[...], embeddings_ref[...], NT).astype(BF)
 
 
-def serve_kernel(table_ref, wanted_ref, out_ref):
+def serve_kernel(table_ref, wanted_ref, out_hbm, out_ref, left):
     numbers = row_numbers()
     groups, rank, slots = out_ref.shape
-    step = 4
-    for first in range(0, groups, step):
+    step = groups // 4
+    copies = []
+    for i in range(4):
+        first = i * step
         index = jnp.concatenate([wanted_ref[first + j] for j in range(step)], axis=1)
         served = dot(table_ref[...], one_hot(index, 0, table_ref.shape[1], numbers)).astype(BF)
         for j in range(step):
             out_ref[first + j] = served[:, j * slots : (j + 1) * slots]
+        some = pl.ds(first, step)
+        copies.append(pltpu.make_async_copy(out_ref.at[some], out_hbm.at[some], left.at[i]))
+        copies[-1].start()
+    for copy in copies:
+        copy.wait()
 
 
 def own_gather_kernel(table_ref, triplets_ref, positive_ref, negative_ref):
@@ -87,27 +94,33 @@
 
 
 def middle_kernel(fetched_ref, triplets_ref, cotangent_ref, positive_hbm, negative_hbm,
-                  remote_ref, pull_hbm, push_hbm,
-                  table_ref, positive_ref, negative_ref, pull_ref, push_ref, arrived, left, *, own):
-    incoming = [pltpu.make_async_copy(positive_hbm, positive_ref, arrived.at[0]),
-                pltpu.make_async_copy(negative_hbm, negative_ref, arrived.at[1])]
+                  remote_hbm, pull_hbm, push_hbm,
+                  table_ref, positive_ref, negative_ref, remote_ref, pull_ref, push_ref,
+                  arrived, left, sent, *, own):
+    numbers = row_numbers()
+    groups, rank, slots = fetched_ref.shape
+    rows = groups * slots
+    count = triplets_ref.shape[1]
+    parts = 4
+    step = count // parts
+    incoming = []
+    for i in range(parts):
+        at = pl.ds(i * step, step)
+        incoming.append([
+            pltpu.make_async_copy(positive_hbm.at[:, at], positive_ref.at[:, at], arrived.at[2 * i]),
+            pltpu.make_async_copy(negative_hbm.at[:, at], negative_ref.at[:, at], arrived.at[2 * i + 1])])
+        for copy in incoming[-1]:
+            copy.start()
     outgoing = [pltpu.make_async_copy(pull_ref, pull_hbm, left.at[0]),
                 pltpu.make_async_copy(push_ref, push_hbm, left.at[1])]
-    for copy in incoming:
-        copy.start()
-    numbers = row_numbers()
-    groups, rank, slots = fetched_ref.shape
-    rows = groups * slots
-    step = 512
     for g in range(groups):
         table_ref[:, g * slots : (g + 1) * slots] = fetched_ref[g]
-    for i in range(0, triplets_ref.shape[1], step):
-        at = pl.ds(i, step)
+    for i in range(parts):
+        at = pl.ds(i * step, step)
         positive = dot(table_ref[...], one_hot(triplets_ref[1:2, at], own, rows, numbers))
         negative = dot(table_ref[...], one_hot(triplets_ref[2:3, at], own, rows, numbers))
-        if i == 0:
-            for copy in incoming:
-                copy.wait()
+        for copy in incoming[i]:
+            copy.wait()
         to_positive = positive_ref[:, at] - positive
         to_negative = negative_ref[:, at] - negative
         near = distance_scale * jnp.sum(to_positive * to_positive, axis=0, keepdims=True)
@@ -120,14 +133,18 @@
         push_ref[:, at] = (push * to_negative).astype(BF)
     for copy in outgoing:
         copy.start()
+    step = rows // parts
     per = step // slots
-    for i in range(rows // step):
+    for i in range(parts):
         base = own + i * step
         total = dot(pull_ref[...], one_hot(triplets_ref[1:2, :], base, step, numbers), NT)
         total = total + dot(push_ref[...], one_hot(triplets_ref[2:3, :], base, step, numbers), NT)
         total = total.astype(BF)
         for j in range(per):
             remote_ref[i * per + j] = total[:, j * slots : (j + 1) * slots]
+        some = pl.ds(i * per, per)
+        outgoing.append(pltpu.make_async_copy(remote_ref.at[some], remote_hbm.at[some], sent.at[i]))
+        outgoing[-1].start()
     for copy in outgoing:
         copy.wait()
 
@@ -144,36 +161,29 @@
         out_ref[:, pl.ds(base, BLOCK)] = dot(pull_ref[...], parts[0], NT) + dot(push_ref[...], parts[1], NT)
 
 
-def finish_kernel(side_ref, own_hbm, returned_ref, wanted_ref, embeddings_hbm,
-                  rounded_ref, kept_ref, sent_ref, back_ref, own_ref, embeddings_ref, arrived):
-    own_copy = pltpu.make_async_copy(own_hbm, own_ref, arrived.at[0])
-    embeddings_copy = pltpu.make_async_copy(embeddings_hbm, embeddings_ref, arrived.at[1])
-    own_copy.start()
+def finish_kernel(own_hbm, returned_ref, wanted_ref, embeddings_hbm,
+                  rounded_ref, partial_ref, back_ref, own_ref, embeddings_ref, arrived):
+    numbers = row_numbers()
+    groups, rank, slots = returned_ref.shape
+    rows = own_ref.shape[1]
+    owns = []
+    for i, base in enumerate(range(0, rows, BLOCK)):
+        at = pl.ds(base, BLOCK)
+        owns.append(pltpu.make_async_copy(own_hbm.at[:, at], own_ref.at[:, at], arrived.at[i + 1]))
+        owns[-1].start()
+    embeddings_copy = pltpu.make_async_copy(embeddings_hbm, embeddings_ref, arrived.at[0])
     embeddings_copy.start()
-    numbers = row_numbers()
-    groups, rank, slots = returned_ref.shape
     for g in range(groups):
         back_ref[:, g * slots : (g + 1) * slots] = returned_ref[g]
     index = jnp.concatenate([wanted_ref[g] for g in range(groups)], axis=1)
-    for base in range(0, own_ref.shape[1], BLOCK):
+    for i, base in enumerate(range(0, rows, BLOCK)):
         at = pl.ds(base, BLOCK)
         total = dot(back_ref[...], one_hot(index, base, BLOCK, numbers), NT)
-        if base == 0:
-            own_copy.wait()
+        owns[i].wait()
         rounded_ref[:, at] = (own_ref[:, at] + total).astype(BF)
     embeddings_copy.wait()
-    half = rank // 2
-    side = side_ref[0]
-    mine = pl.multiple_of(side * half, half)
-    theirs = pl.multiple_of((1 - side) * half, half)
-    sent_ref[...] = dot(rounded_ref[pl.ds(theirs, half), :], embeddings_ref[...])
-    kept_ref[...] = dot(rounded_ref[pl.ds(mine, half), :], embeddings_ref[...])
-
-
-def pair_kernel(kept_ref, received_ref, out_ref):
-    groups, part, width = out_ref.shape
-    total = kept_ref[...] + received_ref[...]
-    out_ref[...] = total.reshape(groups, part, width).astype(BF)
+    partial = dot(rounded_ref[...], embeddings_ref[...])
+    partial_ref[...] = partial.reshape(partial_ref.shape).astype(BF)
 
 
 def spread_kernel(parts_ref, out_ref, *, factor):
@@ -185,17 +195,8 @@
         out_ref[g] = total
 
 
-def join_kernel(side_ref, mine_ref, theirs_ref, out_hbm, left):
-    half = mine_ref.shape[0]
-    side = side_ref[0]
-    copies = []
-    for i, (source, start) in enumerate([(mine_ref, side * half), (theirs_ref, (1 - side) * half)]):
-        target = out_hbm.at[pl.ds(pl.multiple_of(start, half), half), :]
-        copies.append(pltpu.make_async_copy(source, target, left.at[i]))
-    for copy in copies:
-        copy.start()
-    for copy in copies:
-        copy.wait()
+def widen_kernel(parts_ref, out_ref):
+    out_ref[...] = parts_ref[...].astype(F32).reshape(out_ref.shape)
 
 
 NEAR, FAR, PLAIN, SCALAR = "near", "far", "plain", "scalar"
@@ -230,48 +231,49 @@
     members = lax.axis_size("dev")
     cores = 2
     levels = members // cores
-    half = rank // cores
-    part = half // groups
-    side = (lax.axis_index("dev") & 1).astype(jnp.int32).reshape(1)
-    swap = [(i, i ^ 1) for i in range(members)]
+    near = groups * cores
+    part = rank // near
+    level = [[g * members + cores * z + c for g in range(groups) for c in range(cores)] for z in range(levels)]
     column = [[cores * z + c for z in range(levels)] for c in range(cores)]
     factor = 1.0 / math.sqrt(cotangent.shape[0] * groups * members)
     requests = groups * slots
-    two = pltpu.SemaphoreType.DMA((2,))
+    blocks = rows // BLOCK
+
+    def arrivals(n):
+        return pltpu.SemaphoreType.DMA((n,))
 
     wanted = exchange(wanted_rows.reshape(groups, 1, slots), "group")
     table = call(project_kernel, "project", [(NEAR, (rank, rows), BF)],
                  [(NEAR, embeddings), (NEAR, projection)])
-    served = call(serve_kernel, "serve", [(NEAR, (groups, rank, slots), BF)], [(NEAR, table), (NEAR, wanted)])
+    served = call(serve_kernel, "serve", [(FAR, (groups, rank, slots), BF)], [(NEAR, table), (NEAR, wanted)],
+                  [pltpu.VMEM((groups, rank, slots), BF), arrivals(4)])
     fetched = exchange(served, "group")
     positive, negative = call(own_gather_kernel, "own_gather", [(PLAIN, (rank, count), F32)] * 2,
                               [(NEAR, table), (NEAR, triplets)])
     remote, pull, push = call(
         functools.partial(middle_kernel, own=rows), "middle",
-        [(NEAR, (groups, rank, slots), BF), (FAR, (rank, count), BF), (FAR, (rank, count), BF)],
+        [(FAR, (groups, rank, slots), BF), (FAR, (rank, count), BF), (FAR, (rank, count), BF)],
         [(NEAR, fetched), (NEAR, triplets), (NEAR, cotangent.reshape(1, count)), (FAR, positive), (FAR, negative)],
         [pltpu.VMEM((rank, requests), BF)] + [pltpu.VMEM((rank, count), F32)] * 2
-        + [pltpu.VMEM((rank, count), BF)] * 2 + [two, two])
+        + [pltpu.VMEM((groups, rank, slots), BF)] + [pltpu.VMEM((rank, count), BF)] * 2
+        + [arrivals(8), arrivals(2), arrivals(4)])
     returned = exchange(remote, "group")
     own = call(own_scatter_kernel, "own_scatter", [(PLAIN, (rank, rows), F32)],
                [(PLAIN, pull), (PLAIN, push), (NEAR, triplets)])
-    rounded, kept, sent = call(
+    rounded, partial = call(
         finish_kernel, "finish",
-        [(NEAR, (rank, rows), BF), (NEAR, (half, width), F32), (NEAR, (half, width), F32)],
-        [(SCALAR, side), (FAR, own), (NEAR, returned), (NEAR, wanted), (FAR, embeddings)],
-        [pltpu.VMEM((rank, requests), BF), pltpu.VMEM((rank, rows), F32), pltpu.VMEM((rows, width), BF), two])
-    received = lax.ppermute(sent, "dev", swap)
-    chip = call(pair_kernel, "pair", [(NEAR, (groups, part, width), BF)], [(NEAR, kept), (NEAR, received)])
-    chip = exchange(chip, "group")
+        [(NEAR, (rank, rows), BF), (NEAR, (near, part, width), BF)],
+        [(FAR, own), (NEAR, returned), (NEAR, wanted), (FAR, embeddings)],
+        [pltpu.VMEM((rank, requests), BF), pltpu.VMEM((rank, rows), F32), pltpu.VMEM((rows, width), BF),
+         arrivals(blocks + 1)])
+    plane = exchange(partial, ("group", "dev"), level)
     plane = call(functools.partial(spread_kernel, factor=1.0), "plane",
-                 [(NEAR, (levels, part, width), BF)], [(NEAR, chip)])
-    plane = exchange(plane, "dev", column)
+                 [(NEAR, (levels, part, width), BF)], [(NEAR, plane)])
+    whole = exchange(plane, "dev", column)
     whole = call(functools.partial(spread_kernel, factor=factor), "whole",
-                 [(NEAR, (groups, part, width), F32)], [(NEAR, plane)])
-    mine = exchange(whole, "group").reshape(half, width)
-    theirs = lax.ppermute(mine, "dev", swap)
-    weight_grad = call(join_kernel, "join", [(FAR, (rank, width), F32)],
-                       [(SCALAR, side), (NEAR, mine), (NEAR, theirs)], [two])
+                 [(NEAR, (near, part, width), BF)], [(NEAR, whole)])
+    whole = exchange(whole, ("group", "dev"), level)
+    weight_grad = call(widen_kernel, "widen", [(PLAIN, (rank, width), F32)], [(NEAR, whole)])
     row_grad = lax.dot_general(rounded, projection, (((0,), (0,)), ((), ())),
                                preferred_element_type=F32).astype(BF)
     return (row_grad, weight_grad)

time: 139 us -> 136 us (0.978)
  starting transfers between devices: 32.8 us -> 22.6 us
  waiting for transfers between devices: 18.4 us -> 25.3 us
    ppermute x2 -> x0, starting transfers between devices: 17.1 us -> none  [the longest x1 8.76 us: local(): theirs = lax.ppermute(mine, 'dev', swap)]
    all_to_all x3 -> x4, waiting for transfers between devices: 17 us -> 25.3 us  [exchange(): lax.all_to_all(value, axis, split_axis=0, concat_axis=0, tiled=True, axis...]
    all_to_all x3 -> x4, starting transfers between devices: 15.6 us -> 22.6 us  [exchange(): lax.all_to_all(value, axis, split_axis=0, concat_axis=0, tiled=True, axis...]
    pallas_call x10 -> x9, Pallas kernels: 30.8 us -> 31.5 us  [call(): pl.pallas_call(kernel, out_shape=shapes, in_specs=[SPECS[place] for place...]
    all_to_all x3 -> x2, blocking collectives: 51.1 us -> 50.6 us  [exchange(): lax.all_to_all(value, axis, split_axis=0, concat_axis=0, tiled=True, axis...]
  transfers between devices with their start and end apart: 5 -> 4, of which waited for: 4 -> 4; matrix products, arithmetic and copies ran while one was open for 1% -> 1% of each run, Pallas kernels for 8% -> 8%
where the time goes in v3:
time: 136 us; the launch traced here: 135 us
  blocking collectives  50.6 us (37%)
  Pallas kernels  31.5 us (23%)
  waiting for transfers between devices  25.3 us (19%)
  starting transfers between devices  22.6 us (17%)
  local copies, waits for them, and re-layouts  2.55 us (2%)
  matrix products  2 us (1%)
    all_to_all x2, blocking collectives, exchange(): lax.all_to_all(value, axis, split_axis=0, concat_axis=0, tiled=True, axis...  50.6 us
    pallas_call x9, Pallas kernels, call(): pl.pallas_call(kernel, out_shape=shapes, in_specs=[SPECS[place] for place...  31.5 us
    all_to_all x4, waiting for transfers between devices, exchange(): lax.all_to_all(value, axis, split_axis=0, concat_axis=0, tiled=True, axis...  25.3 us
    all_to_all x4, starting transfers between devices, exchange(): lax.all_to_all(value, axis, split_axis=0, concat_axis=0, tiled=True, axis...  22.6 us
  transfers between devices with their start and end apart: 4, of which 4 were waited for; matrix products, arithmetic and copies ran while one was open for 1% of the time, Pallas kernels for 8%

profile of v3, /device:TPU:1, one launch (start us, length us, event | category | flops | bytes accessed | tf_op | source)
XLA Modules:
  0.0 135.4 jit_solution(15977105138345193012)
XLA Ops:
  0.6 7.6 %all-to-all-start = ((s32[16,1,128]{2,1,0:T(1,128)}), s32[16,1,128]{2,1,0:T(1,128)S(1)}, u32[]{:S(2)}, u32[]{:S(2)}) async-start(s32[16,1,128]{2,1,0:T(1,128)} %bitcast.5), calls=%async_computation | async-start | bytes 16384 | tf_op jit(solution)/shard_map/all_to_all | solution.py:223
  8.2 0.0 copy-start
  8.2 1.5 %copy-done = bf16[1280,768]{1,0:T(8,128)(2,1)S(1)} copy-done((bf16[1280,768]{1,0:T(8,128)(2,1)S(1)}, bf16[1280,768]{1,0:T(8,128)(2,1)}, u32[]{:S(2)}) %copy-start) | copy-done | bytes 1966104
  9.8 0.0 copy-start.1
  9.8 1.0 copy-done.1
  10.8 0.7 project.1.table_ref
  11.5 0.0 copy-start.3
  11.5 0.0 copy-start.4
  11.5 3.0 %all-to-all-done.wanted_ref = s32[16,1,128]{2,1,0:T(1,128)S(1)} async-done(((s32[16,1,128]{2,1,0:T(1,128)}), s32[16,1,128]{2,1,0:T(1,128)S(1)}, u32[]{:S(2)}, u32[]{:S(2)}) %all-to-all-start) | async-done | bytes 8224 | tf_op jit(solution)/shard_map/all_to_all | solution.py:223
  14.6 2.3 %serve.1 = bf16[16,256,128]{2,1,0:T(8,128)(2,1)} custom-call(bf16[256,1280]{1,0:T(8,128)(2,1)S(1)} %project.1.table_ref, s32[16,1,128]{2,1,0:T(1,128)S(1)} %all-to-all-done.wanted_ref), custom_call_target="tpu_custom_call" | custom-call | tf_op jit(solution)/shard_map/serve/pallas_call | solution.py:215
  16.8 3.7 %all-to-all-start.1 = ((bf16[16,256,128]{2,1,0:T(8,128)(2,1)}), bf16[16,256,128]{2,1,0:T(8,128)(2,1)S(1)}, u32[]{:S(2)}, u32[]{:S(2)}) async-start(bf16[16,256,128]{2,1,0:T(8,128)(2,1)} %serve.1), calls=%async_computation.1 | async-start | bytes 2097152 | tf_op jit(solution)/shard_map/all_to_all | solution.py:223
  20.5 0.0 copy-done.3
  20.5 4.6 %own_gather.1 = (f32[256,2048]{1,0:T(8,128)}, f32[256,2048]{1,0:T(8,128)}) custom-call(bf16[256,1280]{1,0:T(8,128)(2,1)S(1)} %project.1.table_ref, s32[3,2048]{1,0:T(4,128)S(1)} %copy-done.3), custom_call_target="tpu_custom_call" | custom-call | tf_op jit(solution)/shard_map/own_gather/pallas_call | solution.py:215
  25.1 7.6 %all-to-all-done.1.fetched_ref = bf16[16,256,128]{2,1,0:T(8,128)(2,1)S(1)} async-done(((bf16[16,256,128]{2,1,0:T(8,128)(2,1)}), bf16[16,256,128]{2,1,0:T(8,128)(2,1)S(1)}, u32[]{:S(2)}, u32[]{:S(2)}) %all-to-all-start.1) | async-done | bytes 1048608 | tf_op jit(solution)/shard_map/all_to_all | solution.py:223
  32.7 0.0 copy-done.4
  32.7 11.5 %middle.1 = (bf16[16,256,128]{2,1,0:T(8,128)(2,1)}, bf16[256,2048]{1,0:T(8,128)(2,1)}, bf16[256,2048]{1,0:T(8,128)(2,1)}) custom-call(bf16[16,256,128]{2,1,0:T(8,128)(2,1)S(1)} %all-to-all-done.1.fetched_ref, s32[3,2048]{1,0:T(4,128)S(1)} %copy-done.3, f32[1,2048]{1,0:T(1,128)S(1)} %bitcast.4, f32[256,2048]{1,0:T(8,128)} %get-tuple-element.9.positive_hbm, ...), custom_call_target="tpu_custom_call" | custom-call | tf_op jit(solution)/shard_map/middle/pallas_call | solution.py:215
  44.2 4.4 %all-to-all-start.2 = ((bf16[16,256,128]{2,1,0:T(8,128)(2,1)}), bf16[16,256,128]{2,1,0:T(8,128)(2,1)S(1)}, u32[]{:S(2)}, u32[]{:S(2)}) async-start(bf16[16,256,128]{2,1,0:T(8,128)(2,1)} %get-tuple-element.13), calls=%async_computation.2 | async-start | bytes 2097152 | tf_op jit(solution)/shard_map/all_to_all | solution.py:223
  48.6 5.5 %own_scatter.1.own_hbm = f32[256,1280]{1,0:T(8,128)} custom-call(bf16[256,2048]{1,0:T(8,128)(2,1)} %get-tuple-element.11.pull_ref, bf16[256,2048]{1,0:T(8,128)(2,1)} %get-tuple-element.12.push_ref, s32[3,2048]{1,0:T(4,128)S(1)} %copy-done.3), custom_call_target="tpu_custom_call" | custom-call | tf_op jit(solution)/shard_map/own_scatter/pallas_call | solution.py:215
  54.1 6.3 %all-to-all-done.2.returned_ref = bf16[16,256,128]{2,1,0:T(8,128)(2,1)S(1)} async-done(((bf16[16,256,128]{2,1,0:T(8,128)(2,1)}), bf16[16,256,128]{2,1,0:T(8,128)(2,1)S(1)}, u32[]{:S(2)}, u32[]{:S(2)}) %all-to-all-start.2) | async-done | bytes 1048608 | tf_op jit(solution)/shard_map/all_to_all | solution.py:223
  60.5 5.2 %finish.1 = (bf16[256,1280]{1,0:T(8,128)(2,1)S(1)}, bf16[32,8,768]{2,1,0:T(8,128)(2,1)S(1)}) custom-call(f32[256,1280]{1,0:T(8,128)} %own_scatter.1.own_hbm, bf16[16,256,128]{2,1,0:T(8,128)(2,1)S(1)} %all-to-all-done.2.returned_ref, s32[16,1,128]{2,1,0:T(1,128)S(1)} %all-to-all-done.wanted_ref, bf16[1280,768]{1,0:T(8,128)(2,1)} %embeddings_hbm.1), custom_call_target="tpu_custom_call" | custom-call | tf_op jit(solution)/shard_map/finish/pallas_call | solution.py:215
  65.7 0.0 copy-start.2
  65.7 20.1 %all_to_all.30.parts_ref = bf16[32,8,768]{2,1,0:T(8,128)(2,1)S(1)} all-to-all(bf16[32,8,768]{2,1,0:T(8,128)(2,1)S(1)} %get-tuple-element.15), channel_id=1, replica_groups={{0,1,32,33,64,65,96,97,128,129,160,161,192,193,224,225,256,257,288,289,..., dimensions={0} | all-to-all | bytes 786432 | tf_op jit(solution)/shard_map/all_to_all | solution.py:223
  85.8 0.1 plane.1
  85.9 30.5 %all_to_all.31.parts_ref = bf16[16,8,768]{2,1,0:T(8,128)(2,1)S(1)} all-to-all(bf16[16,8,768]{2,1,0:T(8,128)(2,1)S(1)} %plane.1), channel_id=1, replica_groups={{0,2,4,6,8,10,12,14,16,18,20,22,24,26,28,30},{1,3,5,7,9,11,13,15,17,19,..., dimensions={0} | all-to-all | bytes 393216 | tf_op jit(solution)/shard_map/all_to_all | solution.py:223
  116.4 0.8 whole.1
  117.2 7.0 %all-to-all-start.5 = ((bf16[32,8,768]{2,1,0:T(8,128)(2,1)}), bf16[32,8,768]{2,1,0:T(8,128)(2,1)S(1)}, u32[]{:S(2)}, u32[]{:S(2)}) async-start(bf16[32,8,768]{2,1,0:T(8,128)(2,1)} %whole.1), calls=%async_computation.5 | async-start | bytes 786432 | tf_op jit(solution)/shard_map/all_to_all | solution.py:223
  124.2 0.0 copy-done.2
  124.2 2.0 %convolution_convert_fusion = bf16[1280,768]{1,0:T(8,128)(2,1)} fusion(bf16[256,1280]{1,0:T(8,128)(2,1)S(1)} %get-tuple-element.14, bf16[256,768]{1,0:T(8,128)(2,1)S(1)} %copy-done.2), kind=kOutput, calls=%fused_computation | convolution fusion | flops 504299520 | bytes 3014656 | tf_op jit(solution)/shard_map/dot_general | solution.py:277
  126.2 8.3 %all-to-all-done.5.parts_ref = bf16[32,8,768]{2,1,0:T(8,128)(2,1)S(1)} async-done(((bf16[32,8,768]{2,1,0:T(8,128)(2,1)}), bf16[32,8,768]{2,1,0:T(8,128)(2,1)S(1)}, u32[]{:S(2)}, u32[]{:S(2)}) %all-to-all-start.5) | async-done | bytes 393248 | tf_op jit(solution)/shard_map/all_to_all | solution.py:223
  134.5 0.9 widen.1
Async XLA Ops:
  0.6 13.9 %all-to-all-start = ((s32[16,1,128]{2,1,0:T(1,128)}), s32[16,1,128]{2,1,0:T(1,128)S(1)}, u32[]{:S(2)}, u32[]{:S(2)}) async-start(s32[16,1,128]{2,1,0:T(1,128)} %bitcast.5), calls=%async_computation | async-start | bytes 16384 | tf_op jit(solution)/shard_map/all_to_all | solution.py:223
  8.2 1.5 %copy-start = (bf16[1280,768]{1,0:T(8,128)(2,1)S(1)}, bf16[1280,768]{1,0:T(8,128)(2,1)}, u32[]{:S(2)}) copy-start(bf16[1280,768]{1,0:T(8,128)(2,1)} %embeddings_hbm.1) | copy-start | bytes 5898244
  9.8 1.0 copy-start.1
  11.5 9.0 %copy-start.3 = (s32[3,2048]{1,0:T(4,128)S(1)}, s32[3,2048]{1,0:T(4,128)}, u32[]{:S(2)}) copy-start(s32[3,2048]{1,0:T(4,128)} %triplets_ref.5) | copy-start | bytes 73732
  11.5 21.2 %copy-start.4 = (f32[2048]{0:T(1024)S(1)}, f32[2048]{0:T(1024)}, u32[]{:S(2)}) copy-start(f32[2048]{0:T(1024)} %param.8) | copy-start | bytes 24580
  16.8 15.9 %all-to-all-start.1 = ((bf16[16,256,128]{2,1,0:T(8,128)(2,1)}), bf16[16,256,128]{2,1,0:T(8,128)(2,1)S(1)}, u32[]{:S(2)}, u32[]{:S(2)}) async-start(bf16[16,256,128]{2,1,0:T(8,128)(2,1)} %serve.1), calls=%async_computation.1 | async-start | bytes 2097152 | tf_op jit(solution)/shard_map/all_to_all | solution.py:223
  44.2 16.3 %all-to-all-start.2 = ((bf16[16,256,128]{2,1,0:T(8,128)(2,1)}), bf16[16,256,128]{2,1,0:T(8,128)(2,1)S(1)}, u32[]{:S(2)}, u32[]{:S(2)}) async-start(bf16[16,256,128]{2,1,0:T(8,128)(2,1)} %get-tuple-element.13), calls=%async_computation.2 | async-start | bytes 2097152 | tf_op jit(solution)/shard_map/all_to_all | solution.py:223
  65.7 58.5 %copy-start.2 = (bf16[256,768]{1,0:T(8,128)(2,1)S(1)}, bf16[256,768]{1,0:T(8,128)(2,1)}, u32[]{:S(2)}) copy-start(bf16[256,768]{1,0:T(8,128)(2,1)} %projection_ref.1) | copy-start | bytes 1179652
  117.2 17.3 %all-to-all-start.5 = ((bf16[32,8,768]{2,1,0:T(8,128)(2,1)}), bf16[32,8,768]{2,1,0:T(8,128)(2,1)S(1)}, u32[]{:S(2)}, u32[]{:S(2)}) async-start(bf16[32,8,768]{2,1,0:T(8,128)(2,1)} %whole.1), calls=%async_computation.5 | async-start | bytes 786432 | tf_op jit(solution)/shard_map/all_to_all | solution.py:223

commit v4 on v3

--- a/solution.py
+++ b/solution.py
@@ -45,23 +45,15 @@
     return blocks[0] if len(blocks) == 1 else jnp.concatenate(blocks, axis=0)
 
 
-def difference(anchor, other, rows, numbers):
-    blocks = []
-    for r in range(0, rows, BLOCK):
-        pieces = [
-            select(m, 1.0) - select(n, 1.0)
-            for m, n in zip(hits(anchor, r, numbers), hits(other, r, numbers))
-        ]
-        blocks.append(jnp.concatenate(pieces, axis=1))
-    return jnp.concatenate(blocks, axis=0)
-
-
 def dot(a, b, contract=NN):
     return lax.dot_general(a, b, contract, preferred_element_type=F32)
 
 
-def project_kernel(embeddings_ref, projection_ref, out_ref):
+def project_kernel(embeddings_ref, projection_ref, out_ref, out_hbm, left):
     out_ref[...] = dot(projection_ref[...], embeddings_ref[...], NT).astype(BF)
+    copy = pltpu.make_async_copy(out_ref, out_hbm, left.at[0])
+    copy.start()
+    copy.wait()
 
 
 def serve_kernel(table_ref, wanted_ref, out_hbm, out_ref, left):
@@ -82,20 +74,23 @@
         copy.wait()
 
 
-def own_gather_kernel(table_ref, triplets_ref, positive_ref, negative_ref):
+def own_gather_kernel(table_ref, triplets_ref, anchor_ref, positive_ref, negative_hbm, negative_ref, left):
     numbers = row_numbers()
     rows = table_ref.shape[1]
     step = 512
-    for i in range(0, triplets_ref.shape[1], step):
-        at = pl.ds(i, step)
-        anchor = triplets_ref[0:1, at]
-        positive_ref[:, at] = dot(table_ref[...], difference(anchor, triplets_ref[1:2, at], rows, numbers))
-        negative_ref[:, at] = dot(table_ref[...], difference(anchor, triplets_ref[2:3, at], rows, numbers))
-
-
-def middle_kernel(fetched_ref, triplets_ref, cotangent_ref, positive_hbm, negative_hbm,
+    copy = pltpu.make_async_copy(negative_ref, negative_hbm, left.at[0])
+    for row, out_ref in ((2, negative_ref), (0, anchor_ref), (1, positive_ref)):
+        for i in range(0, triplets_ref.shape[1], step):
+            at = pl.ds(i, step)
+            out_ref[:, at] = dot(table_ref[...], one_hot(triplets_ref[row : row + 1, at], 0, rows, numbers)).astype(BF)
+        if row == 2:
+            copy.start()
+    copy.wait()
+
+
+def middle_kernel(fetched_ref, triplets_ref, cotangent_ref, anchor_ref, positive_ref, negative_hbm,
                   remote_hbm, pull_hbm, push_hbm,
-                  table_ref, positive_ref, negative_ref, remote_ref, pull_ref, push_ref,
+                  table_ref, negative_ref, remote_ref, pull_ref, push_ref,
                   arrived, left, sent, *, own):
     numbers = row_numbers()
     groups, rank, slots = fetched_ref.shape
@@ -103,14 +98,8 @@
     count = triplets_ref.shape[1]
     parts = 4
     step = count // parts
-    incoming = []
-    for i in range(parts):
-        at = pl.ds(i * step, step)
-        incoming.append([
-            pltpu.make_async_copy(positive_hbm.at[:, at], positive_ref.at[:, at], arrived.at[2 * i]),
-            pltpu.make_async_copy(negative_hbm.at[:, at], negative_ref.at[:, at], arrived.at[2 * i + 1])])
-        for copy in incoming[-1]:
-            copy.start()
+    incoming = pltpu.make_async_copy(negative_hbm, negative_ref, arrived.at[0])
+    incoming.start()
     outgoing = [pltpu.make_async_copy(pull_ref, pull_hbm, left.at[0]),
                 pltpu.make_async_copy(push_ref, push_hbm, left.at[1])]
     for g in range(groups):
@@ -119,10 +108,11 @@
         at = pl.ds(i * step, step)
         positive = dot(table_ref[...], one_hot(triplets_ref[1:2, at], own, rows, numbers))
         negative = dot(table_ref[...], one_hot(triplets_ref[2:3, at], own, rows, numbers))
-        for copy in incoming[i]:
-            copy.wait()
-        to_positive = positive_ref[:, at] - positive
-        to_negative = negative_ref[:, at] - negative
+        if i == 0:
+            incoming.wait()
+        anchor = anchor_ref[:, at].astype(F32)
+        to_positive = anchor - (positive_ref[:, at].astype(F32) + positive)
+        to_negative = anchor - (negative_ref[:, at].astype(F32) + negative)
         near = distance_scale * jnp.sum(to_positive * to_positive, axis=0, keepdims=True)
         far = distance_scale * jnp.sum(to_negative * to_negative, axis=0, keepdims=True)
         gate = jax.nn.sigmoid(margin + near - far)
@@ -161,29 +151,25 @@
         out_ref[:, pl.ds(base, BLOCK)] = dot(pull_ref[...], parts[0], NT) + dot(push_ref[...], parts[1], NT)
 
 
-def finish_kernel(own_hbm, returned_ref, wanted_ref, embeddings_hbm,
-                  rounded_ref, partial_ref, back_ref, own_ref, embeddings_ref, arrived):
+def finish_kernel(on_ref, own_ref, returned_ref, wanted_ref, embeddings_hbm,
+                  rounded_ref, partial_ref, back_ref, embeddings_ref, arrived):
     numbers = row_numbers()
     groups, rank, slots = returned_ref.shape
-    rows = own_ref.shape[1]
-    owns = []
-    for i, base in enumerate(range(0, rows, BLOCK)):
-        at = pl.ds(base, BLOCK)
-        owns.append(pltpu.make_async_copy(own_hbm.at[:, at], own_ref.at[:, at], arrived.at[i + 1]))
-        owns[-1].start()
-    embeddings_copy = pltpu.make_async_copy(embeddings_hbm, embeddings_ref, arrived.at[0])
-    embeddings_copy.start()
-    for g in range(groups):
-        back_ref[:, g * slots : (g + 1) * slots] = returned_ref[g]
-    index = jnp.concatenate([wanted_ref[g] for g in range(groups)], axis=1)
-    for i, base in enumerate(range(0, rows, BLOCK)):
-        at = pl.ds(base, BLOCK)
-        total = dot(back_ref[...], one_hot(index, base, BLOCK, numbers), NT)
-        owns[i].wait()
-        rounded_ref[:, at] = (own_ref[:, at] + total).astype(BF)
-    embeddings_copy.wait()
-    partial = dot(rounded_ref[...], embeddings_ref[...])
-    partial_ref[...] = partial.reshape(partial_ref.shape).astype(BF)
+    copy = pltpu.make_async_copy(embeddings_hbm, embeddings_ref, arrived.at[0])
+    copy.start()
+
+    @pl.when(on_ref[0] >= 0)
+    def _():
+        for g in range(groups):
+            back_ref[:, g * slots : (g + 1) * slots] = returned_ref[g]
+        index = jnp.concatenate([wanted_ref[g] for g in range(groups)], axis=1)
+        for base in range(0, own_ref.shape[1], BLOCK):
+            at = pl.ds(base, BLOCK)
+            total = dot(back_ref[...], one_hot(index, base, BLOCK, numbers), NT)
+            rounded_ref[:, at] = (own_ref[:, at] + total).astype(BF)
+
+    copy.wait()
+    partial_ref[...] = dot(rounded_ref[...], embeddings_ref[...]).astype(BF)
 
 
 def spread_kernel(parts_ref, out_ref, *, factor):
@@ -196,7 +182,7 @@
 
 
 def widen_kernel(parts_ref, out_ref):
-    out_ref[...] = parts_ref[...].astype(F32).reshape(out_ref.shape)
+    out_ref[...] = parts_ref[...].astype(F32)
 
 
 NEAR, FAR, PLAIN, SCALAR = "near", "far", "plain", "scalar"
@@ -237,43 +223,44 @@
     column = [[cores * z + c for z in range(levels)] for c in range(cores)]
     factor = 1.0 / math.sqrt(cotangent.shape[0] * groups * members)
     requests = groups * slots
-    blocks = rows // BLOCK
+    on = lax.axis_index("dev").astype(jnp.int32).reshape(1)
 
     def arrivals(n):
         return pltpu.SemaphoreType.DMA((n,))
 
     wanted = exchange(wanted_rows.reshape(groups, 1, slots), "group")
-    table = call(project_kernel, "project", [(NEAR, (rank, rows), BF)],
-                 [(NEAR, embeddings), (NEAR, projection)])
+    table, table_hbm = call(project_kernel, "project", [(NEAR, (rank, rows), BF), (FAR, (rank, rows), BF)],
+                            [(NEAR, embeddings), (NEAR, projection)], [arrivals(1)])
     served = call(serve_kernel, "serve", [(FAR, (groups, rank, slots), BF)], [(NEAR, table), (NEAR, wanted)],
                   [pltpu.VMEM((groups, rank, slots), BF), arrivals(4)])
     fetched = exchange(served, "group")
-    positive, negative = call(own_gather_kernel, "own_gather", [(PLAIN, (rank, count), F32)] * 2,
-                              [(NEAR, table), (NEAR, triplets)])
+    anchor, positive, negative = call(
+        own_gather_kernel, "own_gather",
+        [(NEAR, (rank, count), BF), (NEAR, (rank, count), BF), (FAR, (rank, count), BF)],
+        [(PLAIN, table_hbm), (NEAR, triplets)], [pltpu.VMEM((rank, count), BF), arrivals(1)])
     remote, pull, push = call(
         functools.partial(middle_kernel, own=rows), "middle",
         [(FAR, (groups, rank, slots), BF), (FAR, (rank, count), BF), (FAR, (rank, count), BF)],
-        [(NEAR, fetched), (NEAR, triplets), (NEAR, cotangent.reshape(1, count)), (FAR, positive), (FAR, negative)],
-        [pltpu.VMEM((rank, requests), BF)] + [pltpu.VMEM((rank, count), F32)] * 2
-        + [pltpu.VMEM((groups, rank, slots), BF)] + [pltpu.VMEM((rank, count), BF)] * 2
-        + [arrivals(8), arrivals(2), arrivals(4)])
+        [(NEAR, fetched), (NEAR, triplets), (NEAR, cotangent.reshape(1, count)),
+         (NEAR, anchor), (NEAR, positive), (FAR, negative)],
+        [pltpu.VMEM((rank, requests), BF), pltpu.VMEM((rank, count), BF), pltpu.VMEM((groups, rank, slots), BF)]
+        + [pltpu.VMEM((rank, count), BF)] * 2 + [arrivals(1), arrivals(2), arrivals(4)])
     returned = exchange(remote, "group")
-    own = call(own_scatter_kernel, "own_scatter", [(PLAIN, (rank, rows), F32)],
+    own = call(own_scatter_kernel, "own_scatter", [(NEAR, (rank, rows), F32)],
                [(PLAIN, pull), (PLAIN, push), (NEAR, triplets)])
     rounded, partial = call(
         finish_kernel, "finish",
-        [(NEAR, (rank, rows), BF), (NEAR, (near, part, width), BF)],
-        [(FAR, own), (NEAR, returned), (NEAR, wanted), (FAR, embeddings)],
-        [pltpu.VMEM((rank, requests), BF), pltpu.VMEM((rank, rows), F32), pltpu.VMEM((rows, width), BF),
-         arrivals(blocks + 1)])
-    plane = exchange(partial, ("group", "dev"), level)
+        [(NEAR, (rank, rows), BF), (NEAR, (rank, width), BF)],
+        [(SCALAR, on), (NEAR, own), (NEAR, returned), (NEAR, wanted), (FAR, embeddings)],
+        [pltpu.VMEM((rank, requests), BF), pltpu.VMEM((rows, width), BF), arrivals(1)])
+    plane = exchange(partial.reshape(near, part, width), ("group", "dev"), level)
     plane = call(functools.partial(spread_kernel, factor=1.0), "plane",
                  [(NEAR, (levels, part, width), BF)], [(NEAR, plane)])
     whole = exchange(plane, "dev", column)
     whole = call(functools.partial(spread_kernel, factor=factor), "whole",
                  [(NEAR, (near, part, width), BF)], [(NEAR, whole)])
     whole = exchange(whole, ("group", "dev"), level)
-    weight_grad = call(widen_kernel, "widen", [(PLAIN, (rank, width), F32)], [(NEAR, whole)])
+    weight_grad = call(widen_kernel, "widen", [(PLAIN, (rank, width), F32)], [(NEAR, whole.reshape(rank, width))])
     row_grad = lax.dot_general(rounded, projection, (((0,), (0,)), ((), ())),
                                preferred_element_type=F32).astype(BF)
     return (row_grad, weight_grad)

time: 136 us -> 133 us (0.978)
  blocking collectives: 50.6 us -> 45.7 us
  waiting for transfers between devices: 25.3 us -> 28.2 us
  Pallas kernels: 31.5 us -> 28.8 us
  starting transfers between devices: 22.6 us -> 24.3 us
    all_to_all x2, blocking collectives: 50.6 us -> 45.7 us  [exchange(): lax.all_to_all(value, axis, split_axis=0, concat_axis=0, tiled=True, axis...]
    all_to_all x4, waiting for transfers between devices: 25.3 us -> 28.2 us  [exchange(): lax.all_to_all(value, axis, split_axis=0, concat_axis=0, tiled=True, axis...]
    pallas_call x9, Pallas kernels: 31.5 us -> 28.8 us  [call(): pl.pallas_call(kernel, out_shape=shapes, in_specs=[SPECS[place] for place...]
    all_to_all x4, starting transfers between devices: 22.6 us -> 24.3 us  [exchange(): lax.all_to_all(value, axis, split_axis=0, concat_axis=0, tiled=True, axis...]
  transfers between devices with their start and end apart: 4 -> 4, of which waited for: 4 -> 4; matrix products, arithmetic and copies ran while one was open for 1% -> 2% of each run, Pallas kernels for 8% -> 9%
where the time goes in v4:
time: 133 us; the launch traced here: 132 us
  blocking collectives  45.7 us (34%)
  Pallas kernels  28.8 us (22%)
  waiting for transfers between devices  28.2 us (21%)
  starting transfers between devices  24.3 us (18%)
  local copies, waits for them, and re-layouts  2.55 us (2%)
  matrix products  2 us (2%)
    all_to_all x2, blocking collectives, exchange(): lax.all_to_all(value, axis, split_axis=0, concat_axis=0, tiled=True, axis...  45.7 us
    pallas_call x9, Pallas kernels, call(): pl.pallas_call(kernel, out_shape=shapes, in_specs=[SPECS[place] for place...  28.8 us
    all_to_all x4, waiting for transfers between devices, exchange(): lax.all_to_all(value, axis, split_axis=0, concat_axis=0, tiled=True, axis...  28.2 us
    all_to_all x4, starting transfers between devices, exchange(): lax.all_to_all(value, axis, split_axis=0, concat_axis=0, tiled=True, axis...  24.3 us
  transfers between devices with their start and end apart: 4, of which 4 were waited for; matrix products, arithmetic and copies ran while one was open for 2% of the time, Pallas kernels for 9%

profile of v4, /device:TPU:1, one launch (start us, length us, event | category | flops | bytes accessed | tf_op | source)
XLA Modules:
  0.0 132.3 jit_solution(11590353563389365773)
XLA Ops:
  0.6 7.6 %all-to-all-start = ((s32[16,1,128]{2,1,0:T(1,128)}), s32[16,1,128]{2,1,0:T(1,128)S(1)}, u32[]{:S(2)}, u32[]{:S(2)}) async-start(s32[16,1,128]{2,1,0:T(1,128)} %bitcast.10), calls=%async_computation | async-start | bytes 16384 | tf_op jit(solution)/shard_map/all_to_all | solution.py:209
  8.2 0.0 copy-start
  8.2 1.5 %copy-done = bf16[1280,768]{1,0:T(8,128)(2,1)S(1)} copy-done((bf16[1280,768]{1,0:T(8,128)(2,1)S(1)}, bf16[1280,768]{1,0:T(8,128)(2,1)}, u32[]{:S(2)}) %copy-start) | copy-done | bytes 1966104
  9.8 0.0 copy-start.1
  9.8 1.0 copy-done.1
  10.8 1.6 %project.1 = (bf16[256,1280]{1,0:T(8,128)(2,1)S(1)}, bf16[256,1280]{1,0:T(8,128)(2,1)}) custom-call(bf16[1280,768]{1,0:T(8,128)(2,1)S(1)} %copy-done, bf16[256,768]{1,0:T(8,128)(2,1)S(1)} %copy-done.1), custom_call_target="tpu_custom_call" | custom-call | tf_op jit(solution)/shard_map/project/pallas_call | solution.py:201
  12.3 0.0 copy-start.3
  12.4 2.2 %all-to-all-done.wanted_ref = s32[16,1,128]{2,1,0:T(1,128)S(1)} async-done(((s32[16,1,128]{2,1,0:T(1,128)}), s32[16,1,128]{2,1,0:T(1,128)S(1)}, u32[]{:S(2)}, u32[]{:S(2)}) %all-to-all-start) | async-done | bytes 8224 | tf_op jit(solution)/shard_map/all_to_all | solution.py:209
  14.6 0.0 copy-start.4
  14.6 2.3 %serve.1 = bf16[16,256,128]{2,1,0:T(8,128)(2,1)} custom-call(bf16[256,1280]{1,0:T(8,128)(2,1)S(1)} %get-tuple-element.12.table_ref, s32[16,1,128]{2,1,0:T(1,128)S(1)} %all-to-all-done.wanted_ref), custom_call_target="tpu_custom_call" | custom-call | tf_op jit(solution)/shard_map/serve/pallas_call | solution.py:201
  16.8 4.5 %all-to-all-start.1 = ((bf16[16,256,128]{2,1,0:T(8,128)(2,1)}), bf16[16,256,128]{2,1,0:T(8,128)(2,1)S(1)}, u32[]{:S(2)}, u32[]{:S(2)}) async-start(bf16[16,256,128]{2,1,0:T(8,128)(2,1)} %serve.1), calls=%async_computation.1 | async-start | bytes 2097152 | tf_op jit(solution)/shard_map/all_to_all | solution.py:209
  21.3 0.0 copy-done.3
  21.3 6.0 %own_gather.1 = (bf16[256,2048]{1,0:T(8,128)(2,1)S(1)}, bf16[256,2048]{1,0:T(8,128)(2,1)S(1)}, bf16[256,2048]{1,0:T(8,128)(2,1)}) custom-call(bf16[256,1280]{1,0:T(8,128)(2,1)} %get-tuple-element.13.table_ref, s32[3,2048]{1,0:T(4,128)S(1)} %copy-done.3), custom_call_target="tpu_custom_call" | custom-call | tf_op jit(solution)/shard_map/own_gather/pallas_call | solution.py:201
  27.3 7.8 %all-to-all-done.1.fetched_ref = bf16[16,256,128]{2,1,0:T(8,128)(2,1)S(1)} async-done(((bf16[16,256,128]{2,1,0:T(8,128)(2,1)}), bf16[16,256,128]{2,1,0:T(8,128)(2,1)S(1)}, u32[]{:S(2)}, u32[]{:S(2)}) %all-to-all-start.1) | async-done | bytes 1048608 | tf_op jit(solution)/shard_map/all_to_all | solution.py:209
  35.2 0.0 copy-done.4
  35.2 10.4 %middle.1 = (bf16[16,256,128]{2,1,0:T(8,128)(2,1)}, bf16[256,2048]{1,0:T(8,128)(2,1)}, bf16[256,2048]{1,0:T(8,128)(2,1)}) custom-call(bf16[16,256,128]{2,1,0:T(8,128)(2,1)S(1)} %all-to-all-done.1.fetched_ref, s32[3,2048]{1,0:T(4,128)S(1)} %copy-done.3, f32[1,2048]{1,0:T(1,128)S(1)} %bitcast.9, bf16[256,2048]{1,0:T(8,128)(2,1)S(1)} %get-tuple-element.14.anchor_ref, ...), custom_call_target="tpu_custom_call" | custom-call | tf_op jit(solution)/shard_map/middle/pallas_call | solution.py:201
  45.6 5.3 %all-to-all-start.2 = ((bf16[16,256,128]{2,1,0:T(8,128)(2,1)}), bf16[16,256,128]{2,1,0:T(8,128)(2,1)S(1)}, u32[]{:S(2)}, u32[]{:S(2)}) async-start(bf16[16,256,128]{2,1,0:T(8,128)(2,1)} %get-tuple-element.19), calls=%async_computation.2 | async-start | bytes 2097152 | tf_op jit(solution)/shard_map/all_to_all | solution.py:209
  50.9 4.4 %own_scatter.1.own_ref = f32[256,1280]{1,0:T(8,128)S(1)} custom-call(bf16[256,2048]{1,0:T(8,128)(2,1)} %get-tuple-element.17.pull_ref, bf16[256,2048]{1,0:T(8,128)(2,1)} %get-tuple-element.18.push_ref, s32[3,2048]{1,0:T(4,128)S(1)} %copy-done.3), custom_call_target="tpu_custom_call" | custom-call | tf_op jit(solution)/shard_map/own_scatter/pallas_call | solution.py:201
  55.3 9.9 %all-to-all-done.2.returned_ref = bf16[16,256,128]{2,1,0:T(8,128)(2,1)S(1)} async-done(((bf16[16,256,128]{2,1,0:T(8,128)(2,1)}), bf16[16,256,128]{2,1,0:T(8,128)(2,1)S(1)}, u32[]{:S(2)}, u32[]{:S(2)}) %all-to-all-start.2) | async-done | bytes 1048608 | tf_op jit(solution)/shard_map/all_to_all | solution.py:209
  65.2 2.3 %finish.1 = (bf16[256,1280]{1,0:T(8,128)(2,1)S(1)}, bf16[256,768]{1,0:T(8,128)(2,1)S(1)}) custom-call(s32[1]{0:T(128)} %bitcast.on_ref, f32[256,1280]{1,0:T(8,128)S(1)} %own_scatter.1.own_ref, bf16[16,256,128]{2,1,0:T(8,128)(2,1)S(1)} %all-to-all-done.2.returned_ref, s32[16,1,128]{2,1,0:T(1,128)S(1)} %all-to-all-done.wanted_ref, bf16[1280,768]{1,0:T(8,128)(2,1)} %embeddings_hbm.1), custom_call_target="tpu_custom_call" | custom-call | tf_op jit(solution)/shard_map/finish/pallas_call | solution.py:201
  67.5 0.0 copy-start.2
  67.5 17.6 %all_to_all.30.parts_ref = bf16[32,8,768]{2,1,0:T(8,128)(2,1)S(1)} all-to-all(bf16[32,8,768]{2,1,0:T(8,128)(2,1)S(1)} %bitcast.8), channel_id=1, replica_groups={{0,1,32,33,64,65,96,97,128,129,160,161,192,193,224,225,256,257,288,289,..., dimensions={0} | all-to-all | bytes 786432 | tf_op jit(solution)/shard_map/all_to_all | solution.py:209
  85.1 0.1 plane.1
  85.2 28.1 %all_to_all.31.parts_ref = bf16[16,8,768]{2,1,0:T(8,128)(2,1)S(1)} all-to-all(bf16[16,8,768]{2,1,0:T(8,128)(2,1)S(1)} %plane.1), channel_id=1, replica_groups={{0,2,4,6,8,10,12,14,16,18,20,22,24,26,28,30},{1,3,5,7,9,11,13,15,17,19,..., dimensions={0} | all-to-all | bytes 393216 | tf_op jit(solution)/shard_map/all_to_all | solution.py:209
  113.3 0.8 whole.1
  114.0 7.0 %all-to-all-start.5 = ((bf16[32,8,768]{2,1,0:T(8,128)(2,1)}), bf16[32,8,768]{2,1,0:T(8,128)(2,1)S(1)}, u32[]{:S(2)}, u32[]{:S(2)}) async-start(bf16[32,8,768]{2,1,0:T(8,128)(2,1)} %whole.1), calls=%async_computation.5 | async-start | bytes 786432 | tf_op jit(solution)/shard_map/all_to_all | solution.py:209
  121.0 0.0 copy-done.2
  121.0 2.0 %convolution_convert_fusion = bf16[1280,768]{1,0:T(8,128)(2,1)} fusion(bf16[256,1280]{1,0:T(8,128)(2,1)S(1)} %get-tuple-element.20, bf16[256,768]{1,0:T(8,128)(2,1)S(1)} %copy-done.2), kind=kOutput, calls=%fused_computation | convolution fusion | flops 504299520 | bytes 3014656 | tf_op jit(solution)/shard_map/dot_general | solution.py:264
  123.0 8.3 %all-to-all-done.5 = bf16[32,8,768]{2,1,0:T(8,128)(2,1)S(1)} async-done(((bf16[32,8,768]{2,1,0:T(8,128)(2,1)}), bf16[32,8,768]{2,1,0:T(8,128)(2,1)S(1)}, u32[]{:S(2)}, u32[]{:S(2)}) %all-to-all-start.5) | async-done | bytes 393248 | tf_op jit(solution)/shard_map/all_to_all | solution.py:209
  131.3 0.9 widen.1
Async XLA Ops:
  0.6 13.9 %all-to-all-start = ((s32[16,1,128]{2,1,0:T(1,128)}), s32[16,1,128]{2,1,0:T(1,128)S(1)}, u32[]{:S(2)}, u32[]{:S(2)}) async-start(s32[16,1,128]{2,1,0:T(1,128)} %bitcast.10), calls=%async_computation | async-start | bytes 16384 | tf_op jit(solution)/shard_map/all_to_all | solution.py:209
  8.2 1.5 %copy-start = (bf16[1280,768]{1,0:T(8,128)(2,1)S(1)}, bf16[1280,768]{1,0:T(8,128)(2,1)}, u32[]{:S(2)}) copy-start(bf16[1280,768]{1,0:T(8,128)(2,1)} %embeddings_hbm.1) | copy-start | bytes 5898244
  9.8 1.0 copy-start.1
  12.3 9.0 %copy-start.3 = (s32[3,2048]{1,0:T(4,128)S(1)}, s32[3,2048]{1,0:T(4,128)}, u32[]{:S(2)}) copy-start(s32[3,2048]{1,0:T(4,128)} %triplets_ref.5) | copy-start | bytes 73732
  14.6 20.6 %copy-start.4 = (f32[2048]{0:T(1024)S(1)}, f32[2048]{0:T(1024)}, u32[]{:S(2)}) copy-start(f32[2048]{0:T(1024)} %param.8) | copy-start | bytes 24580
  16.8 18.3 %all-to-all-start.1 = ((bf16[16,256,128]{2,1,0:T(8,128)(2,1)}), bf16[16,256,128]{2,1,0:T(8,128)(2,1)S(1)}, u32[]{:S(2)}, u32[]{:S(2)}) async-start(bf16[16,256,128]{2,1,0:T(8,128)(2,1)} %serve.1), calls=%async_computation.1 | async-start | bytes 2097152 | tf_op jit(solution)/shard_map/all_to_all | solution.py:209
  45.6 19.6 %all-to-all-start.2 = ((bf16[16,256,128]{2,1,0:T(8,128)(2,1)}), bf16[16,256,128]{2,1,0:T(8,128)(2,1)S(1)}, u32[]{:S(2)}, u32[]{:S(2)}) async-start(bf16[16,256,128]{2,1,0:T(8,128)(2,1)} %get-tuple-element.19), calls=%async_computation.2 | async-start | bytes 2097152 | tf_op jit(solution)/shard_map/all_to_all | solution.py:209
  67.5 53.5 %copy-start.2 = (bf16[256,768]{1,0:T(8,128)(2,1)S(1)}, bf16[256,768]{1,0:T(8,128)(2,1)}, u32[]{:S(2)}) copy-start(bf16[256,768]{1,0:T(8,128)(2,1)} %projection_ref.1) | copy-start | bytes 1179652
  114.0 17.3 %all-to-all-start.5 = ((bf16[32,8,768]{2,1,0:T(8,128)(2,1)}), bf16[32,8,768]{2,1,0:T(8,128)(2,1)S(1)}, u32[]{:S(2)}, u32[]{:S(2)}) async-start(bf16[32,8,768]{2,1,0:T(8,128)(2,1)} %whole.1), calls=%async_computation.5 | async-start | bytes 786432 | tf_op jit(solution)/shard_map/all_to_all | solution.py:209

commit v5 on v4

--- a/solution.py
+++ b/solution.py
@@ -15,6 +15,7 @@
 F32 = jnp.float32
 BLOCK = 256
 LANES = 128
+STACK = 2
 NT = (((1,), (1,)), ((), ()))
 NN = (((1,), (0,)), ((), ()))
 PARAMS = pltpu.CompilerParams(vmem_limit_bytes=24 * 1024 * 1024)
@@ -169,7 +170,10 @@
             rounded_ref[:, at] = (own_ref[:, at] + total).astype(BF)
 
     copy.wait()
-    partial_ref[...] = dot(rounded_ref[...], embeddings_ref[...]).astype(BF)
+    partial = dot(rounded_ref[...], embeddings_ref[...]).astype(BF)
+    strip = partial_ref.shape[1]
+    for i in range(partial_ref.shape[0] // rank):
+        partial_ref[i * rank : (i + 1) * rank, :] = partial[:, i * strip : (i + 1) * strip]
 
 
 def spread_kernel(parts_ref, out_ref, *, factor):
@@ -182,7 +186,10 @@
 
 
 def widen_kernel(parts_ref, out_ref):
-    out_ref[...] = parts_ref[...].astype(F32)
+    rank = out_ref.shape[0]
+    strip = parts_ref.shape[1]
+    for i in range(parts_ref.shape[0] // rank):
+        out_ref[:, i * strip : (i + 1) * strip] = parts_ref[i * rank : (i + 1) * rank, :].astype(F32)
 
 
 NEAR, FAR, PLAIN, SCALAR = "near", "far", "plain", "scalar"
@@ -217,10 +224,15 @@
     members = lax.axis_size("dev")
     cores = 2
     levels = members // cores
-    near = groups * cores
-    part = rank // near
-    level = [[g * members + cores * z + c for g in range(groups) for c in range(cores)] for z in range(levels)]
-    column = [[cores * z + c for z in range(levels)] for c in range(cores)]
+    stack = STACK
+    near = groups * cores * stack
+    part = rank // (groups * cores)
+    strip = width // stack
+    level = [
+        [g * members + cores * (z * stack + b) + c for b in range(stack) for g in range(groups) for c in range(cores)]
+        for z in range(levels // stack)]
+    column = [
+        [cores * (z * stack + b) + c for z in range(levels // stack)] for b in range(stack) for c in range(cores)]
     factor = 1.0 / math.sqrt(cotangent.shape[0] * groups * members)
     requests = groups * slots
     on = lax.axis_index("dev").astype(jnp.int32).reshape(1)
@@ -250,17 +262,17 @@
                [(PLAIN, pull), (PLAIN, push), (NEAR, triplets)])
     rounded, partial = call(
         finish_kernel, "finish",
-        [(NEAR, (rank, rows), BF), (NEAR, (rank, width), BF)],
+        [(NEAR, (rank, rows), BF), (NEAR, (rank * stack, strip), BF)],
         [(SCALAR, on), (NEAR, own), (NEAR, returned), (NEAR, wanted), (FAR, embeddings)],
         [pltpu.VMEM((rank, requests), BF), pltpu.VMEM((rows, width), BF), arrivals(1)])
-    plane = exchange(partial.reshape(near, part, width), ("group", "dev"), level)
+    plane = exchange(partial.reshape(near, part, strip), ("group", "dev"), level)
     plane = call(functools.partial(spread_kernel, factor=1.0), "plane",
-                 [(NEAR, (levels, part, width), BF)], [(NEAR, plane)])
+                 [(NEAR, (levels // stack, part, strip), BF)], [(NEAR, plane)])
     whole = exchange(plane, "dev", column)
     whole = call(functools.partial(spread_kernel, factor=factor), "whole",
-                 [(NEAR, (near, part, width), BF)], [(NEAR, whole)])
+                 [(NEAR, (near, part, strip), BF)], [(NEAR, whole)])
     whole = exchange(whole, ("group", "dev"), level)
-    weight_grad = call(widen_kernel, "widen", [(PLAIN, (rank, width), F32)], [(NEAR, whole.reshape(rank, width))])
+    weight_grad = call(widen_kernel, "widen", [(PLAIN, (rank, width), F32)], [(NEAR, whole.reshape(rank * stack, strip))])
     row_grad = lax.dot_general(rounded, projection, (((0,), (0,)), ((), ())),
                                preferred_element_type=F32).astype(BF)
     return (row_grad, weight_grad)

time: 133 us -> 133 us (level)
  no operation moved by 1% of the time
where the time goes in v5:
time: 133 us; the launch traced here: 132 us
  blocking collectives  45.7 us (34%)
  waiting for transfers between devices  28.9 us (22%)
  Pallas kernels  28.8 us (22%)
  starting transfers between devices  23.6 us (18%)
  local copies, waits for them, and re-layouts  2.55 us (2%)
  matrix products  2 us (2%)
    all_to_all x2, blocking collectives, exchange(): lax.all_to_all(value, axis, split_axis=0, concat_axis=0, tiled=True, axis...  45.7 us
    all_to_all x4, waiting for transfers between devices, exchange(): lax.all_to_all(value, axis, split_axis=0, concat_axis=0, tiled=True, axis...  28.9 us
    pallas_call x9, Pallas kernels, call(): pl.pallas_call(kernel, out_shape=shapes, in_specs=[SPECS[place] for place...  28.8 us
    all_to_all x4, starting transfers between devices, exchange(): lax.all_to_all(value, axis, split_axis=0, concat_axis=0, tiled=True, axis...  23.6 us
  transfers between devices with their start and end apart: 4, of which 4 were waited for; matrix products, arithmetic and copies ran while one was open for 2% of the time, Pallas kernels for 9%

profile of v5, /device:TPU:1, one launch (start us, length us, event | category | flops | bytes accessed | tf_op | source)
XLA Modules:
  0.0 132.3 jit_solution(15003013753969664938)
XLA Ops:
  0.6 7.6 %all-to-all-start = ((s32[16,1,128]{2,1,0:T(1,128)}), s32[16,1,128]{2,1,0:T(1,128)S(1)}, u32[]{:S(2)}, u32[]{:S(2)}) async-start(s32[16,1,128]{2,1,0:T(1,128)} %bitcast.10), calls=%async_computation | async-start | bytes 16384 | tf_op jit(solution)/shard_map/all_to_all | solution.py:216
  8.2 0.0 copy-start
  8.2 1.5 %copy-done = bf16[1280,768]{1,0:T(8,128)(2,1)S(1)} copy-done((bf16[1280,768]{1,0:T(8,128)(2,1)S(1)}, bf16[1280,768]{1,0:T(8,128)(2,1)}, u32[]{:S(2)}) %copy-start) | copy-done | bytes 1966104
  9.8 0.0 copy-start.1
  9.8 1.0 copy-done.1
  10.8 1.6 %project.1 = (bf16[256,1280]{1,0:T(8,128)(2,1)S(1)}, bf16[256,1280]{1,0:T(8,128)(2,1)}) custom-call(bf16[1280,768]{1,0:T(8,128)(2,1)S(1)} %copy-done, bf16[256,768]{1,0:T(8,128)(2,1)S(1)} %copy-done.1), custom_call_target="tpu_custom_call" | custom-call | tf_op jit(solution)/shard_map/project/pallas_call | solution.py:208
  12.3 0.0 copy-start.3
  12.4 2.2 %all-to-all-done.wanted_ref = s32[16,1,128]{2,1,0:T(1,128)S(1)} async-done(((s32[16,1,128]{2,1,0:T(1,128)}), s32[16,1,128]{2,1,0:T(1,128)S(1)}, u32[]{:S(2)}, u32[]{:S(2)}) %all-to-all-start) | async-done | bytes 8224 | tf_op jit(solution)/shard_map/all_to_all | solution.py:216
  14.6 0.0 copy-start.4
  14.6 2.3 %serve.1 = bf16[16,256,128]{2,1,0:T(8,128)(2,1)} custom-call(bf16[256,1280]{1,0:T(8,128)(2,1)S(1)} %get-tuple-element.12.table_ref, s32[16,1,128]{2,1,0:T(1,128)S(1)} %all-to-all-done.wanted_ref), custom_call_target="tpu_custom_call" | custom-call | tf_op jit(solution)/shard_map/serve/pallas_call | solution.py:208
  16.8 4.5 %all-to-all-start.1 = ((bf16[16,256,128]{2,1,0:T(8,128)(2,1)}), bf16[16,256,128]{2,1,0:T(8,128)(2,1)S(1)}, u32[]{:S(2)}, u32[]{:S(2)}) async-start(bf16[16,256,128]{2,1,0:T(8,128)(2,1)} %serve.1), calls=%async_computation.1 | async-start | bytes 2097152 | tf_op jit(solution)/shard_map/all_to_all | solution.py:216
  21.3 0.0 copy-done.3
  21.3 6.0 %own_gather.1 = (bf16[256,2048]{1,0:T(8,128)(2,1)S(1)}, bf16[256,2048]{1,0:T(8,128)(2,1)S(1)}, bf16[256,2048]{1,0:T(8,128)(2,1)}) custom-call(bf16[256,1280]{1,0:T(8,128)(2,1)} %get-tuple-element.13.table_ref, s32[3,2048]{1,0:T(4,128)S(1)} %copy-done.3), custom_call_target="tpu_custom_call" | custom-call | tf_op jit(solution)/shard_map/own_gather/pallas_call | solution.py:208
  27.3 7.8 %all-to-all-done.1.fetched_ref = bf16[16,256,128]{2,1,0:T(8,128)(2,1)S(1)} async-done(((bf16[16,256,128]{2,1,0:T(8,128)(2,1)}), bf16[16,256,128]{2,1,0:T(8,128)(2,1)S(1)}, u32[]{:S(2)}, u32[]{:S(2)}) %all-to-all-start.1) | async-done | bytes 1048608 | tf_op jit(solution)/shard_map/all_to_all | solution.py:216
  35.2 0.0 copy-done.4
  35.2 10.4 %middle.1 = (bf16[16,256,128]{2,1,0:T(8,128)(2,1)}, bf16[256,2048]{1,0:T(8,128)(2,1)}, bf16[256,2048]{1,0:T(8,128)(2,1)}) custom-call(bf16[16,256,128]{2,1,0:T(8,128)(2,1)S(1)} %all-to-all-done.1.fetched_ref, s32[3,2048]{1,0:T(4,128)S(1)} %copy-done.3, f32[1,2048]{1,0:T(1,128)S(1)} %bitcast.9, bf16[256,2048]{1,0:T(8,128)(2,1)S(1)} %get-tuple-element.14.anchor_ref, ...), custom_call_target="tpu_custom_call" | custom-call | tf_op jit(solution)/shard_map/middle/pallas_call | solution.py:208
  45.6 5.3 %all-to-all-start.2 = ((bf16[16,256,128]{2,1,0:T(8,128)(2,1)}), bf16[16,256,128]{2,1,0:T(8,128)(2,1)S(1)}, u32[]{:S(2)}, u32[]{:S(2)}) async-start(bf16[16,256,128]{2,1,0:T(8,128)(2,1)} %get-tuple-element.19), calls=%async_computation.2 | async-start | bytes 2097152 | tf_op jit(solution)/shard_map/all_to_all | solution.py:216
  50.9 4.4 %own_scatter.1.own_ref = f32[256,1280]{1,0:T(8,128)S(1)} custom-call(bf16[256,2048]{1,0:T(8,128)(2,1)} %get-tuple-element.17.pull_ref, bf16[256,2048]{1,0:T(8,128)(2,1)} %get-tuple-element.18.push_ref, s32[3,2048]{1,0:T(4,128)S(1)} %copy-done.3), custom_call_target="tpu_custom_call" | custom-call | tf_op jit(solution)/shard_map/own_scatter/pallas_call | solution.py:208
  55.3 9.9 %all-to-all-done.2.returned_ref = bf16[16,256,128]{2,1,0:T(8,128)(2,1)S(1)} async-done(((bf16[16,256,128]{2,1,0:T(8,128)(2,1)}), bf16[16,256,128]{2,1,0:T(8,128)(2,1)S(1)}, u32[]{:S(2)}, u32[]{:S(2)}) %all-to-all-start.2) | async-done | bytes 1048608 | tf_op jit(solution)/shard_map/all_to_all | solution.py:216
  65.2 2.3 %finish.1 = (bf16[256,1280]{1,0:T(8,128)(2,1)S(1)}, bf16[512,384]{1,0:T(8,128)(2,1)S(1)}) custom-call(s32[1]{0:T(128)} %bitcast.on_ref, f32[256,1280]{1,0:T(8,128)S(1)} %own_scatter.1.own_ref, bf16[16,256,128]{2,1,0:T(8,128)(2,1)S(1)} %all-to-all-done.2.returned_ref, s32[16,1,128]{2,1,0:T(1,128)S(1)} %all-to-all-done.wanted_ref, bf16[1280,768]{1,0:T(8,128)(2,1)} %embeddings_hbm.1), custom_call_target="tpu_custom_call" | custom-call | tf_op jit(solution)/shard_map/finish/pallas_call | solution.py:208
  67.5 0.0 copy-start.2
  67.5 20.0 %all_to_all.30.parts_ref = bf16[64,8,384]{2,1,0:T(8,128)(2,1)S(1)} all-to-all(bf16[64,8,384]{2,1,0:T(8,128)(2,1)S(1)} %bitcast.8), channel_id=1, replica_groups={{0,1,32,33,64,65,96,97,128,129,160,161,192,193,224,225,256,257,288,289,..., dimensions={0} | all-to-all | bytes 786432 | tf_op jit(solution)/shard_map/all_to_all | solution.py:216
  87.6 0.1 plane.1
  87.7 25.6 %all_to_all.31.parts_ref = bf16[8,8,384]{2,1,0:T(8,128)(2,1)S(1)} all-to-all(bf16[8,8,384]{2,1,0:T(8,128)(2,1)S(1)} %plane.1), channel_id=1, replica_groups={{0,4,8,12,16,20,24,28},{1,5,9,13,17,21,25,29},{2,6,10,14,18,22,26,30},{..., dimensions={0} | all-to-all | bytes 98304 | tf_op jit(solution)/shard_map/all_to_all | solution.py:216
  113.3 0.8 whole.1
  114.1 6.3 %all-to-all-start.5 = ((bf16[64,8,384]{2,1,0:T(8,128)(2,1)}), bf16[64,8,384]{2,1,0:T(8,128)(2,1)S(1)}, u32[]{:S(2)}, u32[]{:S(2)}) async-start(bf16[64,8,384]{2,1,0:T(8,128)(2,1)} %whole.1), calls=%async_computation.5 | async-start | bytes 786432 | tf_op jit(solution)/shard_map/all_to_all | solution.py:216
  120.4 0.0 copy-done.2
  120.4 2.0 %convolution_convert_fusion = bf16[1280,768]{1,0:T(8,128)(2,1)} fusion(bf16[256,1280]{1,0:T(8,128)(2,1)S(1)} %get-tuple-element.20, bf16[256,768]{1,0:T(8,128)(2,1)S(1)} %copy-done.2), kind=kOutput, calls=%fused_computation | convolution fusion | flops 504299520 | bytes 3014656 | tf_op jit(solution)/shard_map/dot_general | solution.py:276
  122.4 9.0 %all-to-all-done.5 = bf16[64,8,384]{2,1,0:T(8,128)(2,1)S(1)} async-done(((bf16[64,8,384]{2,1,0:T(8,128)(2,1)}), bf16[64,8,384]{2,1,0:T(8,128)(2,1)S(1)}, u32[]{:S(2)}, u32[]{:S(2)}) %all-to-all-start.5) | async-done | bytes 393248 | tf_op jit(solution)/shard_map/all_to_all | solution.py:216
  131.4 0.9 widen.1
Async XLA Ops:
  0.6 13.9 %all-to-all-start = ((s32[16,1,128]{2,1,0:T(1,128)}), s32[16,1,128]{2,1,0:T(1,128)S(1)}, u32[]{:S(2)}, u32[]{:S(2)}) async-start(s32[16,1,128]{2,1,0:T(1,128)} %bitcast.10), calls=%async_computation | async-start | bytes 16384 | tf_op jit(solution)/shard_map/all_to_all | solution.py:216
  8.2 1.5 %copy-start = (bf16[1280,768]{1,0:T(8,128)(2,1)S(1)}, bf16[1280,768]{1,0:T(8,128)(2,1)}, u32[]{:S(2)}) copy-start(bf16[1280,768]{1,0:T(8,128)(2,1)} %embeddings_hbm.1) | copy-start | bytes 5898244
  9.8 1.0 copy-start.1
  12.3 9.0 %copy-start.3 = (s32[3,2048]{1,0:T(4,128)S(1)}, s32[3,2048]{1,0:T(4,128)}, u32[]{:S(2)}) copy-start(s32[3,2048]{1,0:T(4,128)} %triplets_ref.5) | copy-start | bytes 73732
  14.6 20.6 %copy-start.4 = (f32[2048]{0:T(1024)S(1)}, f32[2048]{0:T(1024)}, u32[]{:S(2)}) copy-start(f32[2048]{0:T(1024)} %param.8) | copy-start | bytes 24580
  16.8 18.3 %all-to-all-start.1 = ((bf16[16,256,128]{2,1,0:T(8,128)(2,1)}), bf16[16,256,128]{2,1,0:T(8,128)(2,1)S(1)}, u32[]{:S(2)}, u32[]{:S(2)}) async-start(bf16[16,256,128]{2,1,0:T(8,128)(2,1)} %serve.1), calls=%async_computation.1 | async-start | bytes 2097152 | tf_op jit(solution)/shard_map/all_to_all | solution.py:216
  45.6 19.6 %all-to-all-start.2 = ((bf16[16,256,128]{2,1,0:T(8,128)(2,1)}), bf16[16,256,128]{2,1,0:T(8,128)(2,1)S(1)}, u32[]{:S(2)}, u32[]{:S(2)}) async-start(bf16[16,256,128]{2,1,0:T(8,128)(2,1)} %get-tuple-element.19), calls=%async_computation.2 | async-start | bytes 2097152 | tf_op jit(solution)/shard_map/all_to_all | solution.py:216
  67.5 52.8 %copy-start.2 = (bf16[256,768]{1,0:T(8,128)(2,1)S(1)}, bf16[256,768]{1,0:T(8,128)(2,1)}, u32[]{:S(2)}) copy-start(bf16[256,768]{1,0:T(8,128)(2,1)} %projection_ref.1) | copy-start | bytes 1179652
  114.1 17.3 %all-to-all-start.5 = ((bf16[64,8,384]{2,1,0:T(8,128)(2,1)}), bf16[64,8,384]{2,1,0:T(8,128)(2,1)S(1)}, u32[]{:S(2)}, u32[]{:S(2)}) async-start(bf16[64,8,384]{2,1,0:T(8,128)(2,1)} %whole.1), calls=%async_computation.5 | async-start | bytes 786432 | tf_op jit(solution)/shard_map/all_to_all | solution.py:216

commit v6 on v4

--- a/solution.py
+++ b/solution.py
@@ -152,7 +152,7 @@
 
 
 def finish_kernel(on_ref, own_ref, returned_ref, wanted_ref, embeddings_hbm,
-                  rounded_ref, partial_ref, back_ref, embeddings_ref, arrived):
+                  rounded_ref, partial_hbm, back_ref, embeddings_ref, partial_ref, arrived, left):
     numbers = row_numbers()
     groups, rank, slots = returned_ref.shape
     copy = pltpu.make_async_copy(embeddings_hbm, embeddings_ref, arrived.at[0])
@@ -169,7 +169,15 @@
             rounded_ref[:, at] = (own_ref[:, at] + total).astype(BF)
 
     copy.wait()
-    partial_ref[...] = dot(rounded_ref[...], embeddings_ref[...]).astype(BF)
+    outgoing = []
+    half = rank // 2
+    for i in range(2):
+        at = pl.ds(i * half, half)
+        partial_ref[at, :] = dot(rounded_ref[at, :], embeddings_ref[...]).astype(BF)
+        outgoing.append(pltpu.make_async_copy(partial_ref.at[at], partial_hbm.at[at], left.at[i]))
+        outgoing[-1].start()
+    for copy in outgoing:
+        copy.wait()
 
 
 def spread_kernel(parts_ref, out_ref, *, factor):
@@ -250,10 +258,14 @@
                [(PLAIN, pull), (PLAIN, push), (NEAR, triplets)])
     rounded, partial = call(
         finish_kernel, "finish",
-        [(NEAR, (rank, rows), BF), (NEAR, (rank, width), BF)],
+        [(NEAR, (rank, rows), BF), (FAR, (rank, width), BF)],
         [(SCALAR, on), (NEAR, own), (NEAR, returned), (NEAR, wanted), (FAR, embeddings)],
-        [pltpu.VMEM((rank, requests), BF), pltpu.VMEM((rows, width), BF), arrivals(1)])
+        [pltpu.VMEM((rank, requests), BF), pltpu.VMEM((rows, width), BF), pltpu.VMEM((rank, width), BF),
+         arrivals(1), arrivals(2)])
     plane = exchange(partial.reshape(near, part, width), ("group", "dev"), level)
+    row_grad = lax.dot_general(rounded, projection, (((0,), (0,)), ((), ())),
+                               preferred_element_type=F32).astype(BF)
+    plane, row_grad = lax.optimization_barrier((plane, row_grad))
     plane = call(functools.partial(spread_kernel, factor=1.0), "plane",
                  [(NEAR, (levels, part, width), BF)], [(NEAR, plane)])
     whole = exchange(plane, "dev", column)
@@ -261,8 +273,6 @@
                  [(NEAR, (near, part, width), BF)], [(NEAR, whole)])
     whole = exchange(whole, ("group", "dev"), level)
     weight_grad = call(widen_kernel, "widen", [(PLAIN, (rank, width), F32)], [(NEAR, whole.reshape(rank, width))])
-    row_grad = lax.dot_general(rounded, projection, (((0,), (0,)), ((), ())),
-                               preferred_element_type=F32).astype(BF)
     return (row_grad, weight_grad)
 
 

time: 133 us -> 133 us (level)
  no operation moved by 1% of the time
where the time goes in v6:
time: 133 us; the launch traced here: 132 us
  blocking collectives  45.2 us (34%)
  Pallas kernels  28.7 us (22%)
  waiting for transfers between devices  28.2 us (21%)
  starting transfers between devices  24.7 us (19%)
  local copies, waits for them, and re-layouts  2.55 us (2%)
  matrix products  2 us (2%)
    all_to_all x2, blocking collectives, exchange(): lax.all_to_all(value, axis, split_axis=0, concat_axis=0, tiled=True, axis...  45.2 us
    pallas_call x9, Pallas kernels, call(): pl.pallas_call(kernel, out_shape=shapes, in_specs=[SPECS[place] for place...  28.7 us
    all_to_all x4, waiting for transfers between devices, exchange(): lax.all_to_all(value, axis, split_axis=0, concat_axis=0, tiled=True, axis...  28.2 us
    all_to_all x4, starting transfers between devices, exchange(): lax.all_to_all(value, axis, split_axis=0, concat_axis=0, tiled=True, axis...  24.7 us
  transfers between devices with their start and end apart: 4, of which 4 were waited for; matrix products, arithmetic and copies ran while one was open for 2% of the time, Pallas kernels for 9%

profile of v6, /device:TPU:1, one launch (start us, length us, event | category | flops | bytes accessed | tf_op | source)
XLA Modules:
  0.0 132.1 jit_solution(15838232352361608726)
XLA Ops:
  0.6 7.6 %all-to-all-start = ((s32[16,1,128]{2,1,0:T(1,128)}), s32[16,1,128]{2,1,0:T(1,128)S(1)}, u32[]{:S(2)}, u32[]{:S(2)}) async-start(s32[16,1,128]{2,1,0:T(1,128)} %bitcast.10), calls=%async_computation | async-start | bytes 16384 | tf_op jit(solution)/shard_map/all_to_all | solution.py:217
  8.2 0.0 copy-start
  8.2 1.5 %copy-done = bf16[1280,768]{1,0:T(8,128)(2,1)S(1)} copy-done((bf16[1280,768]{1,0:T(8,128)(2,1)S(1)}, bf16[1280,768]{1,0:T(8,128)(2,1)}, u32[]{:S(2)}) %copy-start) | copy-done | bytes 1966104
  9.8 0.0 copy-start.1
  9.8 1.0 copy-done.1
  10.8 1.6 %project.1 = (bf16[256,1280]{1,0:T(8,128)(2,1)S(1)}, bf16[256,1280]{1,0:T(8,128)(2,1)}) custom-call(bf16[1280,768]{1,0:T(8,128)(2,1)S(1)} %copy-done, bf16[256,768]{1,0:T(8,128)(2,1)S(1)} %copy-done.1), custom_call_target="tpu_custom_call" | custom-call | tf_op jit(solution)/shard_map/project/pallas_call | solution.py:209
  12.3 0.0 copy-start.3
  12.4 2.2 %all-to-all-done.wanted_ref = s32[16,1,128]{2,1,0:T(1,128)S(1)} async-done(((s32[16,1,128]{2,1,0:T(1,128)}), s32[16,1,128]{2,1,0:T(1,128)S(1)}, u32[]{:S(2)}, u32[]{:S(2)}) %all-to-all-start) | async-done | bytes 8224 | tf_op jit(solution)/shard_map/all_to_all | solution.py:217
  14.6 0.0 copy-start.4
  14.6 2.3 %serve.1 = bf16[16,256,128]{2,1,0:T(8,128)(2,1)} custom-call(bf16[256,1280]{1,0:T(8,128)(2,1)S(1)} %get-tuple-element.14.table_ref, s32[16,1,128]{2,1,0:T(1,128)S(1)} %all-to-all-done.wanted_ref), custom_call_target="tpu_custom_call" | custom-call | tf_op jit(solution)/shard_map/serve/pallas_call | solution.py:209
  16.8 4.5 %all-to-all-start.1 = ((bf16[16,256,128]{2,1,0:T(8,128)(2,1)}), bf16[16,256,128]{2,1,0:T(8,128)(2,1)S(1)}, u32[]{:S(2)}, u32[]{:S(2)}) async-start(bf16[16,256,128]{2,1,0:T(8,128)(2,1)} %serve.1), calls=%async_computation.1 | async-start | bytes 2097152 | tf_op jit(solution)/shard_map/all_to_all | solution.py:217
  21.3 0.0 copy-done.3
  21.3 6.0 %own_gather.1 = (bf16[256,2048]{1,0:T(8,128)(2,1)S(1)}, bf16[256,2048]{1,0:T(8,128)(2,1)S(1)}, bf16[256,2048]{1,0:T(8,128)(2,1)}) custom-call(bf16[256,1280]{1,0:T(8,128)(2,1)} %get-tuple-element.15.table_ref, s32[3,2048]{1,0:T(4,128)S(1)} %copy-done.3), custom_call_target="tpu_custom_call" | custom-call | tf_op jit(solution)/shard_map/own_gather/pallas_call | solution.py:209
  27.3 7.8 %all-to-all-done.1.fetched_ref = bf16[16,256,128]{2,1,0:T(8,128)(2,1)S(1)} async-done(((bf16[16,256,128]{2,1,0:T(8,128)(2,1)}), bf16[16,256,128]{2,1,0:T(8,128)(2,1)S(1)}, u32[]{:S(2)}, u32[]{:S(2)}) %all-to-all-start.1) | async-done | bytes 1048608 | tf_op jit(solution)/shard_map/all_to_all | solution.py:217
  35.2 0.0 copy-done.4
  35.2 10.4 %middle.1 = (bf16[16,256,128]{2,1,0:T(8,128)(2,1)}, bf16[256,2048]{1,0:T(8,128)(2,1)}, bf16[256,2048]{1,0:T(8,128)(2,1)}) custom-call(bf16[16,256,128]{2,1,0:T(8,128)(2,1)S(1)} %all-to-all-done.1.fetched_ref, s32[3,2048]{1,0:T(4,128)S(1)} %copy-done.3, f32[1,2048]{1,0:T(1,128)S(1)} %bitcast.8, bf16[256,2048]{1,0:T(8,128)(2,1)S(1)} %get-tuple-element.16.anchor_ref, ...), custom_call_target="tpu_custom_call" | custom-call | tf_op jit(solution)/shard_map/middle/pallas_call | solution.py:209
  45.6 5.3 %all-to-all-start.2 = ((bf16[16,256,128]{2,1,0:T(8,128)(2,1)}), bf16[16,256,128]{2,1,0:T(8,128)(2,1)S(1)}, u32[]{:S(2)}, u32[]{:S(2)}) async-start(bf16[16,256,128]{2,1,0:T(8,128)(2,1)} %get-tuple-element.21), calls=%async_computation.2 | async-start | bytes 2097152 | tf_op jit(solution)/shard_map/all_to_all | solution.py:217
  50.9 4.4 %own_scatter.1.own_ref = f32[256,1280]{1,0:T(8,128)S(1)} custom-call(bf16[256,2048]{1,0:T(8,128)(2,1)} %get-tuple-element.19.pull_ref, bf16[256,2048]{1,0:T(8,128)(2,1)} %get-tuple-element.20.push_ref, s32[3,2048]{1,0:T(4,128)S(1)} %copy-done.3), custom_call_target="tpu_custom_call" | custom-call | tf_op jit(solution)/shard_map/own_scatter/pallas_call | solution.py:209
  55.3 9.9 %all-to-all-done.2.returned_ref = bf16[16,256,128]{2,1,0:T(8,128)(2,1)S(1)} async-done(((bf16[16,256,128]{2,1,0:T(8,128)(2,1)}), bf16[16,256,128]{2,1,0:T(8,128)(2,1)S(1)}, u32[]{:S(2)}, u32[]{:S(2)}) %all-to-all-start.2) | async-done | bytes 1048608 | tf_op jit(solution)/shard_map/all_to_all | solution.py:217
  65.2 0.0 copy-start.2
  65.2 3.0 %finish.1 = (bf16[256,1280]{1,0:T(8,128)(2,1)S(1)}, bf16[256,768]{1,0:T(8,128)(2,1)}) custom-call(s32[1]{0:T(128)} %bitcast.on_ref, f32[256,1280]{1,0:T(8,128)S(1)} %own_scatter.1.own_ref, bf16[16,256,128]{2,1,0:T(8,128)(2,1)S(1)} %all-to-all-done.2.returned_ref, s32[16,1,128]{2,1,0:T(1,128)S(1)} %all-to-all-done.wanted_ref, bf16[1280,768]{1,0:T(8,128)(2,1)} %embeddings_hbm.1), custom_call_target="tpu_custom_call" | custom-call | tf_op jit(solution)/shard_map/finish/pallas_call | solution.py:209
  68.2 7.3 %all-to-all-start.3 = ((bf16[32,8,768]{2,1,0:T(8,128)(2,1)}), bf16[32,8,768]{2,1,0:T(8,128)(2,1)S(1)}, u32[]{:S(2)}, u32[]{:S(2)}) async-start(bf16[32,8,768]{2,1,0:T(8,128)(2,1)} %bitcast.9), calls=%async_computation.3 | async-start | bytes 786432 | tf_op jit(solution)/shard_map/all_to_all | solution.py:217
  75.6 0.0 copy-done.2
  75.6 2.0 %convolution_convert_fusion = bf16[1280,768]{1,0:T(8,128)(2,1)} fusion(bf16[256,1280]{1,0:T(8,128)(2,1)S(1)} %get-tuple-element.23, bf16[256,768]{1,0:T(8,128)(2,1)S(1)} %copy-done.2), kind=kOutput, calls=%fused_computation | convolution fusion | flops 504299520 | bytes 3014656 | tf_op jit(solution)/shard_map/dot_general | solution.py:266
  77.6 8.3 %all-to-all-done.3.parts_ref = bf16[32,8,768]{2,1,0:T(8,128)(2,1)S(1)} async-done(((bf16[32,8,768]{2,1,0:T(8,128)(2,1)}), bf16[32,8,768]{2,1,0:T(8,128)(2,1)S(1)}, u32[]{:S(2)}, u32[]{:S(2)}) %all-to-all-start.3) | async-done | bytes 393248 | tf_op jit(solution)/shard_map/all_to_all | solution.py:217
  85.9 0.1 plane.1
  86.0 28.1 %all_to_all.30.parts_ref = bf16[16,8,768]{2,1,0:T(8,128)(2,1)S(1)} all-to-all(bf16[16,8,768]{2,1,0:T(8,128)(2,1)S(1)} %plane.1), channel_id=1, replica_groups={{0,2,4,6,8,10,12,14,16,18,20,22,24,26,28,30},{1,3,5,7,9,11,13,15,17,19,..., dimensions={0} | all-to-all | bytes 393216 | tf_op jit(solution)/shard_map/all_to_all | solution.py:217
  114.1 17.1 %all_to_all.31 = bf16[32,8,768]{2,1,0:T(8,128)(2,1)S(1)} all-to-all(bf16[32,8,768]{2,1,0:T(8,128)(2,1)S(1)} %whole.1), channel_id=1, replica_groups={{0,1,32,33,64,65,96,97,128,129,160,161,192,193,224,225,256,257,288,289,..., dimensions={0} | all-to-all | bytes 786432 | tf_op jit(solution)/shard_map/all_to_all | solution.py:217
  131.2 0.9 widen.1
  (1 shorter events, 0.0 us)
Async XLA Ops:
  0.6 13.9 %all-to-all-start = ((s32[16,1,128]{2,1,0:T(1,128)}), s32[16,1,128]{2,1,0:T(1,128)S(1)}, u32[]{:S(2)}, u32[]{:S(2)}) async-start(s32[16,1,128]{2,1,0:T(1,128)} %bitcast.10), calls=%async_computation | async-start | bytes 16384 | tf_op jit(solution)/shard_map/all_to_all | solution.py:217
  8.2 1.5 %copy-start = (bf16[1280,768]{1,0:T(8,128)(2,1)S(1)}, bf16[1280,768]{1,0:T(8,128)(2,1)}, u32[]{:S(2)}) copy-start(bf16[1280,768]{1,0:T(8,128)(2,1)} %embeddings_hbm.1) | copy-start | bytes 5898244
  9.8 1.0 copy-start.1
  12.3 9.0 %copy-start.3 = (s32[3,2048]{1,0:T(4,128)S(1)}, s32[3,2048]{1,0:T(4,128)}, u32[]{:S(2)}) copy-start(s32[3,2048]{1,0:T(4,128)} %triplets_ref.5) | copy-start | bytes 73732
  14.6 20.6 %copy-start.4 = (f32[2048]{0:T(1024)S(1)}, f32[2048]{0:T(1024)}, u32[]{:S(2)}) copy-start(f32[2048]{0:T(1024)} %param.8) | copy-start | bytes 24580
  16.8 18.3 %all-to-all-start.1 = ((bf16[16,256,128]{2,1,0:T(8,128)(2,1)}), bf16[16,256,128]{2,1,0:T(8,128)(2,1)S(1)}, u32[]{:S(2)}, u32[]{:S(2)}) async-start(bf16[16,256,128]{2,1,0:T(8,128)(2,1)} %serve.1), calls=%async_computation.1 | async-start | bytes 2097152 | tf_op jit(solution)/shard_map/all_to_all | solution.py:217
  45.6 19.6 %all-to-all-start.2 = ((bf16[16,256,128]{2,1,0:T(8,128)(2,1)}), bf16[16,256,128]{2,1,0:T(8,128)(2,1)S(1)}, u32[]{:S(2)}, u32[]{:S(2)}) async-start(bf16[16,256,128]{2,1,0:T(8,128)(2,1)} %get-tuple-element.21), calls=%async_computation.2 | async-start | bytes 2097152 | tf_op jit(solution)/shard_map/all_to_all | solution.py:217
  65.2 10.4 %copy-start.2 = (bf16[256,768]{1,0:T(8,128)(2,1)S(1)}, bf16[256,768]{1,0:T(8,128)(2,1)}, u32[]{:S(2)}) copy-start(bf16[256,768]{1,0:T(8,128)(2,1)} %projection_ref.1) | copy-start | bytes 1179652
  68.2 17.7 %all-to-all-start.3 = ((bf16[32,8,768]{2,1,0:T(8,128)(2,1)}), bf16[32,8,768]{2,1,0:T(8,128)(2,1)S(1)}, u32[]{:S(2)}, u32[]{:S(2)}) async-start(bf16[32,8,768]{2,1,0:T(8,128)(2,1)} %bitcast.9), calls=%async_computation.3 | async-start | bytes 786432 | tf_op jit(solution)/shard_map/all_to_all | solution.py:217

commit v7 on v5

--- a/solution.py
+++ b/solution.py
@@ -153,7 +153,7 @@
 
 
 def finish_kernel(on_ref, own_ref, returned_ref, wanted_ref, embeddings_hbm,
-                  rounded_ref, partial_ref, back_ref, embeddings_ref, arrived):
+                  rounded_ref, partial_hbm, back_ref, embeddings_ref, partial_ref, arrived, left):
     numbers = row_numbers()
     groups, rank, slots = returned_ref.shape
     copy = pltpu.make_async_copy(embeddings_hbm, embeddings_ref, arrived.at[0])
@@ -170,10 +170,15 @@
             rounded_ref[:, at] = (own_ref[:, at] + total).astype(BF)
 
     copy.wait()
-    partial = dot(rounded_ref[...], embeddings_ref[...]).astype(BF)
+    outgoing = []
     strip = partial_ref.shape[1]
     for i in range(partial_ref.shape[0] // rank):
-        partial_ref[i * rank : (i + 1) * rank, :] = partial[:, i * strip : (i + 1) * strip]
+        at = pl.ds(i * rank, rank)
+        partial_ref[at, :] = dot(rounded_ref[...], embeddings_ref[:, i * strip : (i + 1) * strip]).astype(BF)
+        outgoing.append(pltpu.make_async_copy(partial_ref.at[at], partial_hbm.at[at], left.at[i]))
+        outgoing[-1].start()
+    for copy in outgoing:
+        copy.wait()
 
 
 def spread_kernel(parts_ref, out_ref, *, factor):
@@ -262,10 +267,14 @@
                [(PLAIN, pull), (PLAIN, push), (NEAR, triplets)])
     rounded, partial = call(
         finish_kernel, "finish",
-        [(NEAR, (rank, rows), BF), (NEAR, (rank * stack, strip), BF)],
+        [(NEAR, (rank, rows), BF), (FAR, (rank * stack, strip), BF)],
         [(SCALAR, on), (NEAR, own), (NEAR, returned), (NEAR, wanted), (FAR, embeddings)],
-        [pltpu.VMEM((rank, requests), BF), pltpu.VMEM((rows, width), BF), arrivals(1)])
+        [pltpu.VMEM((rank, requests), BF), pltpu.VMEM((rows, width), BF), pltpu.VMEM((rank * stack, strip), BF),
+         arrivals(1), arrivals(2)])
     plane = exchange(partial.reshape(near, part, strip), ("group", "dev"), level)
+    row_grad = lax.dot_general(rounded, projection, (((0,), (0,)), ((), ())),
+                               preferred_element_type=F32).astype(BF)
+    plane, row_grad = lax.optimization_barrier((plane, row_grad))
     plane = call(functools.partial(spread_kernel, factor=1.0), "plane",
                  [(NEAR, (levels // stack, part, strip), BF)], [(NEAR, plane)])
     whole = exchange(plane, "dev", column)
@@ -273,8 +282,6 @@
                  [(NEAR, (near, part, strip), BF)], [(NEAR, whole)])
     whole = exchange(whole, ("group", "dev"), level)
     weight_grad = call(widen_kernel, "widen", [(PLAIN, (rank, width), F32)], [(NEAR, whole.reshape(rank * stack, strip))])
-    row_grad = lax.dot_general(rounded, projection, (((0,), (0,)), ((), ())),
-                               preferred_element_type=F32).astype(BF)
     return (row_grad, weight_grad)
 
 

time: 133 us -> 133 us (level)
  blocking collectives: 45.7 us -> 42.3 us
  starting transfers between devices: 23.6 us -> 26.6 us
    all_to_all x2, blocking collectives: 45.7 us -> 42.3 us  [exchange(): lax.all_to_all(value, axis, split_axis=0, concat_axis=0, tiled=True, axis...]
    all_to_all x4, starting transfers between devices: 23.6 us -> 26.6 us  [exchange(): lax.all_to_all(value, axis, split_axis=0, concat_axis=0, tiled=True, axis...]
where the time goes in v7:
time: 133 us; the launch traced here: 132 us
  blocking collectives  42.3 us (32%)
  Pallas kernels  28.9 us (22%)
  waiting for transfers between devices  28.8 us (22%)
  starting transfers between devices  26.6 us (20%)
  local copies, waits for them, and re-layouts  2.55 us (2%)
  matrix products  2 us (2%)
    all_to_all x2, blocking collectives, exchange(): lax.all_to_all(value, axis, split_axis=0, concat_axis=0, tiled=True, axis...  42.3 us
    pallas_call x9, Pallas kernels, call(): pl.pallas_call(kernel, out_shape=shapes, in_specs=[SPECS[place] for place...  28.9 us
    all_to_all x4, waiting for transfers between devices, exchange(): lax.all_to_all(value, axis, split_axis=0, concat_axis=0, tiled=True, axis...  28.8 us
    all_to_all x4, starting transfers between devices, exchange(): lax.all_to_all(value, axis, split_axis=0, concat_axis=0, tiled=True, axis...  26.6 us
  transfers between devices with their start and end apart: 4, of which 4 were waited for; matrix products, arithmetic and copies ran while one was open for 2% of the time, Pallas kernels for 9%

profile of v7, /device:TPU:1, one launch (start us, length us, event | category | flops | bytes accessed | tf_op | source)
XLA Modules:
  0.0 131.9 jit_solution(13307630864500807952)
XLA Ops:
  0.6 7.6 %all-to-all-start = ((s32[16,1,128]{2,1,0:T(1,128)}), s32[16,1,128]{2,1,0:T(1,128)S(1)}, u32[]{:S(2)}, u32[]{:S(2)}) async-start(s32[16,1,128]{2,1,0:T(1,128)} %bitcast.10), calls=%async_computation | async-start | bytes 16384 | tf_op jit(solution)/shard_map/all_to_all | solution.py:221
  8.2 0.0 copy-start
  8.2 1.5 %copy-done = bf16[1280,768]{1,0:T(8,128)(2,1)S(1)} copy-done((bf16[1280,768]{1,0:T(8,128)(2,1)S(1)}, bf16[1280,768]{1,0:T(8,128)(2,1)}, u32[]{:S(2)}) %copy-start) | copy-done | bytes 1966104
  9.8 0.0 copy-start.1
  9.8 1.0 copy-done.1
  10.8 1.6 %project.1 = (bf16[256,1280]{1,0:T(8,128)(2,1)S(1)}, bf16[256,1280]{1,0:T(8,128)(2,1)}) custom-call(bf16[1280,768]{1,0:T(8,128)(2,1)S(1)} %copy-done, bf16[256,768]{1,0:T(8,128)(2,1)S(1)} %copy-done.1), custom_call_target="tpu_custom_call" | custom-call | tf_op jit(solution)/shard_map/project/pallas_call | solution.py:213
  12.3 0.0 copy-start.3
  12.4 2.2 %all-to-all-done.wanted_ref = s32[16,1,128]{2,1,0:T(1,128)S(1)} async-done(((s32[16,1,128]{2,1,0:T(1,128)}), s32[16,1,128]{2,1,0:T(1,128)S(1)}, u32[]{:S(2)}, u32[]{:S(2)}) %all-to-all-start) | async-done | bytes 8224 | tf_op jit(solution)/shard_map/all_to_all | solution.py:221
  14.6 0.0 copy-start.4
  14.6 2.3 %serve.1 = bf16[16,256,128]{2,1,0:T(8,128)(2,1)} custom-call(bf16[256,1280]{1,0:T(8,128)(2,1)S(1)} %get-tuple-element.14.table_ref, s32[16,1,128]{2,1,0:T(1,128)S(1)} %all-to-all-done.wanted_ref), custom_call_target="tpu_custom_call" | custom-call | tf_op jit(solution)/shard_map/serve/pallas_call | solution.py:213
  16.8 4.5 %all-to-all-start.1 = ((bf16[16,256,128]{2,1,0:T(8,128)(2,1)}), bf16[16,256,128]{2,1,0:T(8,128)(2,1)S(1)}, u32[]{:S(2)}, u32[]{:S(2)}) async-start(bf16[16,256,128]{2,1,0:T(8,128)(2,1)} %serve.1), calls=%async_computation.1 | async-start | bytes 2097152 | tf_op jit(solution)/shard_map/all_to_all | solution.py:221
  21.3 0.0 copy-done.3
  21.3 6.0 %own_gather.1 = (bf16[256,2048]{1,0:T(8,128)(2,1)S(1)}, bf16[256,2048]{1,0:T(8,128)(2,1)S(1)}, bf16[256,2048]{1,0:T(8,128)(2,1)}) custom-call(bf16[256,1280]{1,0:T(8,128)(2,1)} %get-tuple-element.15.table_ref, s32[3,2048]{1,0:T(4,128)S(1)} %copy-done.3), custom_call_target="tpu_custom_call" | custom-call | tf_op jit(solution)/shard_map/own_gather/pallas_call | solution.py:213
  27.3 7.8 %all-to-all-done.1.fetched_ref = bf16[16,256,128]{2,1,0:T(8,128)(2,1)S(1)} async-done(((bf16[16,256,128]{2,1,0:T(8,128)(2,1)}), bf16[16,256,128]{2,1,0:T(8,128)(2,1)S(1)}, u32[]{:S(2)}, u32[]{:S(2)}) %all-to-all-start.1) | async-done | bytes 1048608 | tf_op jit(solution)/shard_map/all_to_all | solution.py:221
  35.2 0.0 copy-done.4
  35.2 10.4 %middle.1 = (bf16[16,256,128]{2,1,0:T(8,128)(2,1)}, bf16[256,2048]{1,0:T(8,128)(2,1)}, bf16[256,2048]{1,0:T(8,128)(2,1)}) custom-call(bf16[16,256,128]{2,1,0:T(8,128)(2,1)S(1)} %all-to-all-done.1.fetched_ref, s32[3,2048]{1,0:T(4,128)S(1)} %copy-done.3, f32[1,2048]{1,0:T(1,128)S(1)} %bitcast.8, bf16[256,2048]{1,0:T(8,128)(2,1)S(1)} %get-tuple-element.16.anchor_ref, ...), custom_call_target="tpu_custom_call" | custom-call | tf_op jit(solution)/shard_map/middle/pallas_call | solution.py:213
  45.6 5.3 %all-to-all-start.2 = ((bf16[16,256,128]{2,1,0:T(8,128)(2,1)}), bf16[16,256,128]{2,1,0:T(8,128)(2,1)S(1)}, u32[]{:S(2)}, u32[]{:S(2)}) async-start(bf16[16,256,128]{2,1,0:T(8,128)(2,1)} %get-tuple-element.21), calls=%async_computation.2 | async-start | bytes 2097152 | tf_op jit(solution)/shard_map/all_to_all | solution.py:221
  50.9 4.4 %own_scatter.1.own_ref = f32[256,1280]{1,0:T(8,128)S(1)} custom-call(bf16[256,2048]{1,0:T(8,128)(2,1)} %get-tuple-element.19.pull_ref, bf16[256,2048]{1,0:T(8,128)(2,1)} %get-tuple-element.20.push_ref, s32[3,2048]{1,0:T(4,128)S(1)} %copy-done.3), custom_call_target="tpu_custom_call" | custom-call | tf_op jit(solution)/shard_map/own_scatter/pallas_call | solution.py:213
  55.3 9.9 %all-to-all-done.2.returned_ref = bf16[16,256,128]{2,1,0:T(8,128)(2,1)S(1)} async-done(((bf16[16,256,128]{2,1,0:T(8,128)(2,1)}), bf16[16,256,128]{2,1,0:T(8,128)(2,1)S(1)}, u32[]{:S(2)}, u32[]{:S(2)}) %all-to-all-start.2) | async-done | bytes 1048608 | tf_op jit(solution)/shard_map/all_to_all | solution.py:221
  65.2 0.0 copy-start.2
  65.2 3.2 %finish.1 = (bf16[256,1280]{1,0:T(8,128)(2,1)S(1)}, bf16[512,384]{1,0:T(8,128)(2,1)}) custom-call(s32[1]{0:T(128)} %bitcast.on_ref, f32[256,1280]{1,0:T(8,128)S(1)} %own_scatter.1.own_ref, bf16[16,256,128]{2,1,0:T(8,128)(2,1)S(1)} %all-to-all-done.2.returned_ref, s32[16,1,128]{2,1,0:T(1,128)S(1)} %all-to-all-done.wanted_ref, bf16[1280,768]{1,0:T(8,128)(2,1)} %embeddings_hbm.1), custom_call_target="tpu_custom_call" | custom-call | tf_op jit(solution)/shard_map/finish/pallas_call | solution.py:213
  68.4 9.2 %all-to-all-start.3 = ((bf16[64,8,384]{2,1,0:T(8,128)(2,1)}), bf16[64,8,384]{2,1,0:T(8,128)(2,1)S(1)}, u32[]{:S(2)}, u32[]{:S(2)}) async-start(bf16[64,8,384]{2,1,0:T(8,128)(2,1)} %bitcast.9), calls=%async_computation.3 | async-start | bytes 786432 | tf_op jit(solution)/shard_map/all_to_all | solution.py:221
  77.6 0.0 copy-done.2
  77.6 2.0 %convolution_convert_fusion = bf16[1280,768]{1,0:T(8,128)(2,1)} fusion(bf16[256,1280]{1,0:T(8,128)(2,1)S(1)} %get-tuple-element.23, bf16[256,768]{1,0:T(8,128)(2,1)S(1)} %copy-done.2), kind=kOutput, calls=%fused_computation | convolution fusion | flops 504299520 | bytes 3014656 | tf_op jit(solution)/shard_map/dot_general | solution.py:275
  79.6 8.9 %all-to-all-done.3.parts_ref = bf16[64,8,384]{2,1,0:T(8,128)(2,1)S(1)} async-done(((bf16[64,8,384]{2,1,0:T(8,128)(2,1)}), bf16[64,8,384]{2,1,0:T(8,128)(2,1)S(1)}, u32[]{:S(2)}, u32[]{:S(2)}) %all-to-all-start.3) | async-done | bytes 393248 | tf_op jit(solution)/shard_map/all_to_all | solution.py:221
  88.5 0.1 plane.1
  88.6 25.6 %all_to_all.30.parts_ref = bf16[8,8,384]{2,1,0:T(8,128)(2,1)S(1)} all-to-all(bf16[8,8,384]{2,1,0:T(8,128)(2,1)S(1)} %plane.1), channel_id=1, replica_groups={{0,4,8,12,16,20,24,28},{1,5,9,13,17,21,25,29},{2,6,10,14,18,22,26,30},{..., dimensions={0} | all-to-all | bytes 98304 | tf_op jit(solution)/shard_map/all_to_all | solution.py:221
  114.3 16.7 %all_to_all.31 = bf16[64,8,384]{2,1,0:T(8,128)(2,1)S(1)} all-to-all(bf16[64,8,384]{2,1,0:T(8,128)(2,1)S(1)} %whole.1), channel_id=1, replica_groups={{0,1,32,33,64,65,96,97,128,129,160,161,192,193,224,225,256,257,288,289,..., dimensions={0} | all-to-all | bytes 786432 | tf_op jit(solution)/shard_map/all_to_all | solution.py:221
  131.0 0.9 widen.1
  (1 shorter events, 0.0 us)
Async XLA Ops:
  0.6 13.9 %all-to-all-start = ((s32[16,1,128]{2,1,0:T(1,128)}), s32[16,1,128]{2,1,0:T(1,128)S(1)}, u32[]{:S(2)}, u32[]{:S(2)}) async-start(s32[16,1,128]{2,1,0:T(1,128)} %bitcast.10), calls=%async_computation | async-start | bytes 16384 | tf_op jit(solution)/shard_map/all_to_all | solution.py:221
  8.2 1.5 %copy-start = (bf16[1280,768]{1,0:T(8,128)(2,1)S(1)}, bf16[1280,768]{1,0:T(8,128)(2,1)}, u32[]{:S(2)}) copy-start(bf16[1280,768]{1,0:T(8,128)(2,1)} %embeddings_hbm.1) | copy-start | bytes 5898244
  9.8 1.0 copy-start.1
  12.3 9.0 %copy-start.3 = (s32[3,2048]{1,0:T(4,128)S(1)}, s32[3,2048]{1,0:T(4,128)}, u32[]{:S(2)}) copy-start(s32[3,2048]{1,0:T(4,128)} %triplets_ref.5) | copy-start | bytes 73732
  14.6 20.6 %copy-start.4 = (f32[2048]{0:T(1024)S(1)}, f32[2048]{0:T(1024)}, u32[]{:S(2)}) copy-start(f32[2048]{0:T(1024)} %param.8) | copy-start | bytes 24580
  16.8 18.3 %all-to-all-start.1 = ((bf16[16,256,128]{2,1,0:T(8,128)(2,1)}), bf16[16,256,128]{2,1,0:T(8,128)(2,1)S(1)}, u32[]{:S(2)}, u32[]{:S(2)}) async-start(bf16[16,256,128]{2,1,0:T(8,128)(2,1)} %serve.1), calls=%async_computation.1 | async-start | bytes 2097152 | tf_op jit(solution)/shard_map/all_to_all | solution.py:221
  45.6 19.6 %all-to-all-start.2 = ((bf16[16,256,128]{2,1,0:T(8,128)(2,1)}), bf16[16,256,128]{2,1,0:T(8,128)(2,1)S(1)}, u32[]{:S(2)}, u32[]{:S(2)}) async-start(bf16[16,256,128]{2,1,0:T(8,128)(2,1)} %get-tuple-element.21), calls=%async_computation.2 | async-start | bytes 2097152 | tf_op jit(solution)/shard_map/all_to_all | solution.py:221
  65.2 12.4 %copy-start.2 = (bf16[256,768]{1,0:T(8,128)(2,1)S(1)}, bf16[256,768]{1,0:T(8,128)(2,1)}, u32[]{:S(2)}) copy-start(bf16[256,768]{1,0:T(8,128)(2,1)} %projection_ref.1) | copy-start | bytes 1179652
  68.4 20.1 %all-to-all-start.3 = ((bf16[64,8,384]{2,1,0:T(8,128)(2,1)}), bf16[64,8,384]{2,1,0:T(8,128)(2,1)S(1)}, u32[]{:S(2)}, u32[]{:S(2)}) async-start(bf16[64,8,384]{2,1,0:T(8,128)(2,1)} %bitcast.9), calls=%async_computation.3 | async-start | bytes 786432 | tf_op jit(solution)/shard_map/all_to_all | solution.py:221
